TPU v7x, 32 devices: a whole 2x2x4 slice. The times are simulated.
32 devices in a mesh: fsdp: 8 (over z, core), dp: 4 (over y, x).
Axes of the slice: x: 2, y: 2, z: 4, core: 2. Of those that a mesh axis runs over, the one named last changes fastest.
Arguments:
- embedded: bfloat16 [2, 1024, 32, 768], P(None, ('fsdp', 'dp')), may hold values from -6 to 6
- first_drop: int32 [2, 1024, 32, 768], P(None, ('fsdp', 'dp')), may hold values 0 or 1
- second_drop: int32 [2, 1024, 32, 768], P(None, ('fsdp', 'dp')), may hold values 0 or 1
- sent_lengths: int32 [1024], P(('fsdp', 'dp')), may hold values from 1 to 32, as said below
- out_cotangent: bfloat16 [2, 1024, 32, 768], P(None, ('fsdp', 'dp')), may hold values from -6 to 6
- triple_weight: bfloat16 [768, 2304], P(('fsdp', 'dp')), may hold values from -0.21875 to 0.21875
- query_value_bias: bfloat16 [1536], P(('fsdp', 'dp')), may hold values from -1.5 to 1.5
- mixer_weight: bfloat16 [768, 768], P(('fsdp', 'dp')), may hold values from -0.875 to 0.875
- mixer_bias: bfloat16 [768], P(('fsdp', 'dp')), may hold values from -1.5 to 1.5
- first_gain: bfloat16 [768], P(('fsdp', 'dp')), may hold values from 0.5 to 1.5
- first_shift: bfloat16 [768], P(('fsdp', 'dp')), may hold values from -1.5 to 1.5
- widen_weight: bfloat16 [768, 3072], P(('fsdp', 'dp')), may hold values from -0.21875 to 0.21875
- widen_bias: bfloat16 [3072], P(('fsdp', 'dp')), may hold values from -1.5 to 1.5
- narrow_weight: bfloat16 [3072, 768], P(('fsdp', 'dp')), may hold values from -0.109375 to 0.109375
- narrow_bias: bfloat16 [768], P(('fsdp', 'dp')), may hold values from -1.5 to 1.5
- second_gain: bfloat16 [768], P(('fsdp', 'dp')), may hold values from 0.5 to 1.5
- second_shift: bfloat16 [768], P(('fsdp', 'dp')), may hold values from -1.5 to 1.5
- pooler_weight: bfloat16 [768, 768], P(('fsdp', 'dp')), may hold values from -0.21875 to 0.21875
- pooler_bias: bfloat16 [768], P(('fsdp', 'dp')), may hold values from -1.5 to 1.5
Outputs:
- loss: float32 [], replicated
- outputs: bfloat16 [2, 1024, 32, 768], P(None, ('fsdp', 'dp'))
- input_grad: bfloat16 [2, 1024, 32, 768], P(None, ('fsdp', 'dp'))
- rms_stats: float32 [3], replicated
- grad_triple_weight: float32 [768, 2304], P(('fsdp', 'dp'))
- grad_query_value_bias: float32 [1536], P(('fsdp', 'dp'))
- grad_mixer_weight: float32 [768, 768], P(('fsdp', 'dp'))
- grad_mixer_bias: float32 [768], P(('fsdp', 'dp'))
- grad_first_gain: float32 [768], P(('fsdp', 'dp'))
- grad_first_shift: float32 [768], P(('fsdp', 'dp'))
- grad_widen_weight: float32 [768, 3072], P(('fsdp', 'dp'))
- grad_widen_bias: float32 [3072], P(('fsdp', 'dp'))
- grad_narrow_weight: float32 [3072, 768], P(('fsdp', 'dp'))
- grad_narrow_bias: float32 [768], P(('fsdp', 'dp'))
- grad_second_gain: float32 [768], P(('fsdp', 'dp'))
- grad_second_shift: float32 [768], P(('fsdp', 'dp'))
- grad_pooler_weight: float32 [768, 768], P(('fsdp', 'dp'))
- grad_pooler_bias: float32 [768], P(('fsdp', 'dp'))
Inputs may be any that keep to these rules, and one draw needn't show every extreme that they name: `sent_lengths`: the sentences of one device lie in a bucket of lengths b - 32 // 4 + 1 to b, where b lies between 8 and 32 ; the first sentence of each device has length b, and some device has b = 32.
All inputs are finite; a program needn't handle non-finite values. No bound on the sum of `first_drop` or of `second_drop` on one device may be relied on, other than what follows from the above.
Results may differ from a plain program's by a relative error of at most 0.014.
Values may be sent and summed in bfloat16 or wider, within the bound.
No kernel may reach another device: no remote copies, remote signals or barrier semaphores. Data moves between devices by JAX's collectives and lax.ppermute only.
A program may use at most 384 MiB of HBM per device.

v0:
```python
import jax
import jax.numpy as jnp
from jax import lax
from jax.sharding import PartitionSpec as P

HEADS = 12


DROP_SCALE = 1.0 / 0.9
SOFTMAX_TEMP = 0.05


def layer_norm(values, norm_gain, norm_shift):
    centred = values - jnp.mean(values, axis=-1, keepdims=True)
    spread = jnp.mean(centred * centred, axis=-1, keepdims=True)
    return centred * lax.rsqrt(spread + 1e-12) * norm_gain + norm_shift


def gelu_exact(values):
    return jax.nn.gelu(values, approximate=False)


def pool_unit(pooler_input):
    pooled = jnp.tanh(pooler_input)
    return pooled * lax.rsqrt(jnp.sum(pooled * pooled, axis=-1, keepdims=True) + 1e-06)


def rows_product(left_side, right_side):
    return lax.dot_general(
        left_side, right_side, (((0,), (0,)), ((), ())), preferred_element_type=jnp.float32
    )


def times_transpose(left_side, right_side):
    return lax.dot_general(
        left_side, right_side, (((1,), (1,)), ((), ())), preferred_element_type=jnp.float32
    )


def column_sums(values):
    return jnp.sum(values, axis=0, dtype=jnp.float32)


def on_device(
    embedded,
    first_drop,
    second_drop,
    sent_lengths,
    out_cotangent,
    triple_weight,
    query_value_bias,
    mixer_weight,
    mixer_bias,
    first_gain,
    first_shift,
    widen_weight,
    widen_bias,
    narrow_weight,
    narrow_bias,
    second_gain,
    second_shift,
    pooler_weight,
    pooler_bias,
):
    view_count, sent_count, length, model_width = embedded.shape
    head_count = HEADS
    head_width = model_width // head_count
    seq_count = view_count * sent_count
    row_count = seq_count * length
    scale_inner = head_width ** (-0.5)
    triple, query_value, mixer, mixer_shift, gain_one, shift_one = (
        lax.all_gather(triple_weight, ("fsdp", "dp"), axis=0, tiled=True),
        lax.all_gather(query_value_bias, ("fsdp", "dp"), axis=0, tiled=True),
        lax.all_gather(mixer_weight, ("fsdp", "dp"), axis=0, tiled=True),
        lax.all_gather(mixer_bias, ("fsdp", "dp"), axis=0, tiled=True),
        lax.all_gather(first_gain, ("fsdp", "dp"), axis=0, tiled=True),
        lax.all_gather(first_shift, ("fsdp", "dp"), axis=0, tiled=True),
    )
    valid_bool = lax.iota(jnp.int32, length)[None, :] < sent_lengths[:, None]
    valid_mask = valid_bool.astype(jnp.float32)
    valid_rows = jnp.broadcast_to(valid_mask[None], (view_count, sent_count, length)).reshape(
        row_count, 1
    )
    valid_keys = jnp.tile(valid_bool, (view_count, 1))
    row_data = embedded.reshape(row_count, model_width)
    drop_one = first_drop.reshape(row_count, model_width).astype(jnp.float32) * DROP_SCALE
    drop_two = second_drop.reshape(row_count, model_width).astype(jnp.float32) * DROP_SCALE
    query_value_f = query_value.astype(jnp.float32)
    bias_full = jnp.concatenate(
        [
            query_value_f[:model_width],
            jnp.zeros((model_width,), jnp.float32),
            query_value_f[model_width:],
        ]
    )
    packed = (jnp.dot(row_data, triple, preferred_element_type=jnp.float32) + bias_full).astype(
        jnp.bfloat16
    )
    packed = packed.reshape(seq_count, length, 3, head_count, head_width)
    queries = packed[:, :, 0]
    key_rows = packed[:, :, 1]
    values = packed[:, :, 2]
    scores = (
        jnp.einsum("sqhe,skhe->shqk", queries, key_rows, preferred_element_type=jnp.float32)
        * scale_inner
    )
    scores = jnp.where(valid_keys[:, None, None, :], scores, -1000000000.0)
    attention = jax.nn.softmax(scores, axis=-1)
    attention_low = attention.astype(jnp.bfloat16)
    context = jnp.einsum(
        "shqk,skhe->sqhe", attention_low, values, preferred_element_type=jnp.float32
    )
    context = context.reshape(row_count, model_width).astype(jnp.bfloat16)
    branch = jnp.dot(context, mixer, preferred_element_type=jnp.float32) + mixer_shift.astype(
        jnp.float32
    )
    attn_part = branch * drop_one
    input_rows = row_data.astype(jnp.float32)
    residual = input_rows + attn_part
    hidden, norm_one_back = jax.vjp(
        layer_norm, residual, gain_one.astype(jnp.float32), shift_one.astype(jnp.float32)
    )
    hidden_low = hidden.astype(jnp.bfloat16)
    widen, widen_shift, narrow, narrow_shift, gain_two, shift_two, pooler, pooler_shift = (
        lax.all_gather(widen_weight, ("fsdp", "dp"), axis=0, tiled=True),
        lax.all_gather(widen_bias, ("fsdp", "dp"), axis=0, tiled=True),
        lax.all_gather(narrow_weight, ("fsdp", "dp"), axis=0, tiled=True),
        lax.all_gather(narrow_bias, ("fsdp", "dp"), axis=0, tiled=True),
        lax.all_gather(second_gain, ("fsdp", "dp"), axis=0, tiled=True),
        lax.all_gather(second_shift, ("fsdp", "dp"), axis=0, tiled=True),
        lax.all_gather(pooler_weight, ("fsdp", "dp"), axis=0, tiled=True),
        lax.all_gather(pooler_bias, ("fsdp", "dp"), axis=0, tiled=True),
    )
    widened = jnp.dot(hidden_low, widen, preferred_element_type=jnp.float32) + widen_shift.astype(
        jnp.float32
    )
    active_f, gelu_back = jax.vjp(gelu_exact, widened)
    active = active_f.astype(jnp.bfloat16)
    narrowed = jnp.dot(active, narrow, preferred_element_type=jnp.float32) + narrow_shift.astype(
        jnp.float32
    )
    ffn_part = narrowed * drop_two
    second = hidden + ffn_part
    normed, norm_two_back = jax.vjp(
        layer_norm, second, gain_two.astype(jnp.float32), shift_two.astype(jnp.float32)
    )
    outputs = (normed * valid_rows).astype(jnp.bfloat16)
    first_token = outputs.reshape(view_count, sent_count, length, model_width)[:, :, 0].reshape(
        seq_count, model_width
    )
    pooler_input = jnp.dot(
        first_token, pooler, preferred_element_type=jnp.float32
    ) + pooler_shift.astype(jnp.float32)
    unit_f, pool_back = jax.vjp(pool_unit, pooler_input)
    unit_rows = unit_f.astype(jnp.bfloat16).reshape(view_count, sent_count, model_width)
    first_unit = unit_rows[0]
    second_unit = unit_rows[1]
    every_second = lax.all_gather(second_unit, ("fsdp", "dp"), axis=0, tiled=True)
    sentence_total = every_second.shape[0]
    cosine_similarity = times_transpose(first_unit, every_second)
    scaled_logits = cosine_similarity / SOFTMAX_TEMP
    log_total = jax.nn.logsumexp(scaled_logits, axis=-1)
    own_columns = lax.axis_index(("fsdp", "dp")) * sent_count + lax.iota(jnp.int32, sent_count)
    target_indicator = (
        lax.iota(jnp.int32, sentence_total)[None, :] == own_columns[:, None]
    ).astype(jnp.float32)
    positive = jnp.sum(target_indicator * scaled_logits, axis=-1)
    loss_part = jnp.sum(log_total - positive)
    square_sums = jnp.stack(
        [
            jnp.sum(valid_rows * input_rows * input_rows),
            jnp.sum(valid_rows * attn_part * attn_part),
            jnp.sum(valid_rows * ffn_part * ffn_part),
            2.0 * jnp.sum(sent_lengths).astype(jnp.float32),
        ]
    )
    loss_total, sums_total = lax.psum((loss_part, square_sums), ("fsdp", "dp"))
    loss_value = loss_total / sentence_total
    rms_stats = jnp.sqrt(sums_total[:3] / (sums_total[3] * model_width))
    softmax_probs = jnp.exp(scaled_logits - log_total[:, None])
    similarity_grad = ((softmax_probs - target_indicator) / SOFTMAX_TEMP).astype(jnp.bfloat16)
    dfirst = jnp.dot(similarity_grad, every_second, preferred_element_type=jnp.float32)
    dsecond_all = rows_product(similarity_grad, first_unit)
    dsecond_unit = lax.psum_scatter(dsecond_all, ("fsdp", "dp"), scatter_dimension=0, tiled=True)
    widen_back, narrow_back, pooler_back = (
        lax.all_gather(widen_weight, ("fsdp", "dp"), axis=0, tiled=True),
        lax.all_gather(narrow_weight, ("fsdp", "dp"), axis=0, tiled=True),
        lax.all_gather(pooler_weight, ("fsdp", "dp"), axis=0, tiled=True),
    )
    dunit = jnp.concatenate([dfirst, dsecond_unit], axis=0)
    dpooler = pool_back(dunit)[0].astype(jnp.bfloat16)
    grad_pooler_weight = rows_product(first_token, dpooler)
    grad_pooler_bias = column_sums(dpooler)
    dfirst_token = times_transpose(dpooler, pooler_back).reshape(
        view_count, sent_count, model_width
    )
    dnormed = out_cotangent.astype(jnp.float32)
    dnormed = dnormed.at[:, :, 0].add(dfirst_token).reshape(row_count, model_width) * valid_rows
    dsecond, grad_second_gain, grad_second_shift = norm_two_back(dnormed)
    dnarrow = (dsecond * drop_two).astype(jnp.bfloat16)
    grad_narrow_weight = rows_product(active, dnarrow)
    grad_narrow_bias = column_sums(dnarrow)
    dactive = times_transpose(dnarrow, narrow_back)
    dwidened = gelu_back(dactive)[0].astype(jnp.bfloat16)
    grad_widen_weight = rows_product(hidden_low, dwidened)
    grad_widen_bias = column_sums(dwidened)
    dhidden = dsecond + times_transpose(dwidened, widen_back)
    ffn_grads = (
        lax.psum_scatter(grad_widen_weight, ("fsdp", "dp"), scatter_dimension=0, tiled=True),
        lax.psum_scatter(grad_widen_bias, ("fsdp", "dp"), scatter_dimension=0, tiled=True),
        lax.psum_scatter(grad_narrow_weight, ("fsdp", "dp"), scatter_dimension=0, tiled=True),
        lax.psum_scatter(grad_narrow_bias, ("fsdp", "dp"), scatter_dimension=0, tiled=True),
        lax.psum_scatter(grad_second_gain, ("fsdp", "dp"), scatter_dimension=0, tiled=True),
        lax.psum_scatter(grad_second_shift, ("fsdp", "dp"), scatter_dimension=0, tiled=True),
        lax.psum_scatter(grad_pooler_weight, ("fsdp", "dp"), scatter_dimension=0, tiled=True),
        lax.psum_scatter(grad_pooler_bias, ("fsdp", "dp"), scatter_dimension=0, tiled=True),
    )
    triple_back, mixer_back = (
        lax.all_gather(triple_weight, ("fsdp", "dp"), axis=0, tiled=True),
        lax.all_gather(mixer_weight, ("fsdp", "dp"), axis=0, tiled=True),
    )
    dresidual, grad_first_gain, grad_first_shift = norm_one_back(dhidden)
    dbranch = (dresidual * drop_one).astype(jnp.bfloat16)
    grad_mixer_weight = rows_product(context, dbranch)
    grad_mixer_bias = column_sums(dbranch)
    dcontext = (
        times_transpose(dbranch, mixer_back)
        .astype(jnp.bfloat16)
        .reshape(seq_count, length, head_count, head_width)
    )
    dattention = jnp.einsum("sqhe,skhe->shqk", dcontext, values, preferred_element_type=jnp.float32)
    dvalues = jnp.einsum(
        "shqk,sqhe->skhe", attention_low, dcontext, preferred_element_type=jnp.float32
    )
    dscores = (
        attention * (dattention - jnp.sum(attention * dattention, axis=-1, keepdims=True))
    ).astype(jnp.bfloat16)
    dqueries = (
        jnp.einsum("shqk,skhe->sqhe", dscores, key_rows, preferred_element_type=jnp.float32)
        * scale_inner
    )
    dkey_rows = (
        jnp.einsum("shqk,sqhe->skhe", dscores, queries, preferred_element_type=jnp.float32)
        * scale_inner
    )
    dpacked = (
        jnp.stack([dqueries, dkey_rows, dvalues], axis=2)
        .astype(jnp.bfloat16)
        .reshape(row_count, 3 * model_width)
    )
    grad_triple_weight = rows_product(row_data, dpacked)
    packed_sums = column_sums(dpacked)
    grad_query_value_bias = jnp.concatenate(
        [packed_sums[:model_width], packed_sums[2 * model_width :]]
    )
    input_grad = (
        (dresidual + times_transpose(dpacked, triple_back))
        .astype(jnp.bfloat16)
        .reshape(embedded.shape)
    )
    attn_grads = (
        lax.psum_scatter(grad_triple_weight, ("fsdp", "dp"), scatter_dimension=0, tiled=True),
        lax.psum_scatter(grad_query_value_bias, ("fsdp", "dp"), scatter_dimension=0, tiled=True),
        lax.psum_scatter(grad_mixer_weight, ("fsdp", "dp"), scatter_dimension=0, tiled=True),
        lax.psum_scatter(grad_mixer_bias, ("fsdp", "dp"), scatter_dimension=0, tiled=True),
        lax.psum_scatter(grad_first_gain, ("fsdp", "dp"), scatter_dimension=0, tiled=True),
        lax.psum_scatter(grad_first_shift, ("fsdp", "dp"), scatter_dimension=0, tiled=True),
    )
    outputs = outputs.reshape(embedded.shape)
    return (
        loss_value,
        outputs,
        input_grad,
        rms_stats,
        attn_grads[0],
        attn_grads[1],
        attn_grads[2],
        attn_grads[3],
        attn_grads[4],
        attn_grads[5],
        ffn_grads[0],
        ffn_grads[1],
        ffn_grads[2],
        ffn_grads[3],
        ffn_grads[4],
        ffn_grads[5],
        ffn_grads[6],
        ffn_grads[7],
    )


def solution(mesh):
    in_specs = (
        P(None, ("fsdp", "dp"), None, None),
        P(None, ("fsdp", "dp"), None, None),
        P(None, ("fsdp", "dp"), None, None),
        P(("fsdp", "dp")),
        P(None, ("fsdp", "dp"), None, None),
        P(("fsdp", "dp"), None),
        P(("fsdp", "dp")),
        P(("fsdp", "dp"), None),
        P(("fsdp", "dp")),
        P(("fsdp", "dp")),
        P(("fsdp", "dp")),
        P(("fsdp", "dp"), None),
        P(("fsdp", "dp")),
        P(("fsdp", "dp"), None),
        P(("fsdp", "dp")),
        P(("fsdp", "dp")),
        P(("fsdp", "dp")),
        P(("fsdp", "dp"), None),
        P(("fsdp", "dp")),
    )
    out_specs = (
        P(),
        P(None, ("fsdp", "dp"), None, None),
        P(None, ("fsdp", "dp"), None, None),
        P(),
        P(("fsdp", "dp"), None),
        P(("fsdp", "dp")),
        P(("fsdp", "dp"), None),
        P(("fsdp", "dp")),
        P(("fsdp", "dp")),
        P(("fsdp", "dp")),
        P(("fsdp", "dp"), None),
        P(("fsdp", "dp")),
        P(("fsdp", "dp"), None),
        P(("fsdp", "dp")),
        P(("fsdp", "dp")),
        P(("fsdp", "dp")),
        P(("fsdp", "dp"), None),
        P(("fsdp", "dp")),
    )
    return jax.shard_map(
        on_device, mesh=mesh, in_specs=in_specs, out_specs=out_specs, check_vma=False
    )
```

profile of v0, /device:TPU:0, one launch (start us, length us, event | category | flops | bytes accessed | tf_op | source)
XLA Modules:
  0.0 1161.4 jit_solution(15726885025658911073)
XLA Ops:
  18.2 42.6 %all-reduce.19 = (bf16[1536]{0:T(1024)(128)(2,1)S(1)}, bf16[768]{0:T(1024)(128)(2,1)S(1)}, bf16[768]{0:T(1024)(128)(2,1)S(1)}, bf16[768]{0:T(1024)(128)(2,1)S(1)...) all-reduce(bf16[1536]{0:T(1024)(128)(2,1)S(1)} %dynamic-update-slic, ...), channel_id=1, replica_groups=mesh['fsdp'=8,'dp'=4] {'fsdp','dp'}, use_global_device_ids=true, to_apply=%add | all-reduce | flops 9984 | bytes 39936
  78.3 11.8 %add_convert_fusion.1 = bf16[2048,2304]{1,0:T(8,128)(2,1)} fusion(bf16[2048,768]{1,0:T(8,128)(2,1)S(1)} %bitcast.108, bf16[768,2304]{1,0:T(8,128)(2,1)} %all-gather.7.cloned.1.call-done, f32[2304]{0:T(1024)S(1)} %pad_maximum_fusion.1), kind=kOutput, calls=%fused_computation.21 | convolution fusion | flops 7257194496 | bytes 16131072 | tf_op jit(solution)/shard_map/dot_general | solution.py:96
  90.1 28.7 %reshape.277 = bf16[64,32,3,12,64]{4,3,2,1,0:T(8,128)(2,1)} reshape(bf16[2048,2304]{1,0:T(8,128)(2,1)} %add_convert_fusion.1) | data formatting | bytes 18874368 | tf_op jit(solution)/shard_map/reshape | solution.py:99
  118.8 17.1 %fusion.57 = (bf16[64,32,1,12,64]{4,3,2,1,0:T(8,128)(2,1)}, bf16[64,32,1,12,64]{4,3,2,1,0:T(8,128)(2,1)}, bf16[64,32,1,12,64]{4,3,2,1,0:T(8,128)(2,1)}) fusion(bf16[64,32,3,12,64]{4,3,2,1,0:T(8,128)(2,1)} %reshape.277), kind=kLoop, calls=%fused_computation.134 | loop fusion | bytes 18874368 | tf_op jit(solution)/shard_map/slice | solution.py:101
  136.0 13.9 %fusion.22 = f32[64,12,32,32]{2,3,1,0:T(8,128)} fusion(bf16[64,32,1,12,64]{4,3,2,1,0:T(8,128)(2,1)} %get-tuple-element.136, bf16[64,32,1,12,64]{4,3,2,1,0:T(8,128)(2,1)} %get-tuple-element.135), kind=kOutput, calls=%fused_computation.75 | convolution fusion | flops 100663296 | bytes 9437184 | tf_op jit(solution)/shard_map/sqhe,skhe->shqk/dot_general | solution.py:104
  149.9 16.3 %fusion.60 = (f32[64,12,32]{2,1,0:T(8,128)S(1)}, f32[64,12,32,32]{2,3,1,0:T(8,128)}) fusion(f32[64,12,32,32]{2,3,1,0:T(8,128)} %fusion.22, pred[64,32]{1,0:T(8,128)(4,1)S(1)} %bitcast.115), kind=kOutput, calls=%fused_computation.137 | output fusion | flops 4718623 | bytes 6391808 | tf_op jit(solution)/shard_map/sub | solution.py:108
  166.1 11.4 convert_bitcast_fusion
  177.5 11.3 copy.62
  188.8 11.5 convert_element_type.145
  200.4 10.2 fusion.56
  214.7 70.2 %multiply_convert_fusion = (bf16[2048,3072]{1,0:T(8,128)(2,1)}, f32[2048,3072]{1,0:T(8,128)}, f32[2048,3072]{1,0:T(8,128)}) fusion(f32[3072]{0:T(1024)S(1)} %convert_element_type.151, bf16[768,3072]{1,0:T(8,128)(2,1)} %all-gather.11.cloned.1.call-done, f32[2048,768]{1,0:T(8,128)} %copy-done.2, f32[768]{0:T(1024)S(1)} %convert_element_type.149, ...), kind=kOutput, calls=%fused_computation.7 | convolution fusion | flops 10086776832 | bytes 73959424 | tf_op jit(solution)/shard_map/dot_general | solution.py:134
  284.9 19.6 %fusion.53 = (f32[2048]{0:T(1024)S(1)}, f32[2048,768]{1,0:T(8,128)S(1)}, f32[2048,768]{1,0:T(8,128)}) fusion(f32[768]{0:T(1024)S(1)} %convert_element_type.149, f32[768]{0:T(1024)S(1)} %convert_element_type.148, f32[2048]{0:T(1024)S(1)} %fusion.38, f32[2048,768]{1,0:T(8,128)} %copy-done.2, f32[2048]{0:T(1024)S(1)} %broadcast_multiply_fusion.1, ...), kind=kOutput, calls=%fused_computation.132 | convolution fusion | flops 9676257280 | bytes 42501120 | tf_op jit(solution)/shard_map/dot_general | solution.py:139
  318.6 54.8 %all-gather.17.cloned.1.call-done = bf16[1024,768]{1,0:T(8,128)(2,1)} async-done(((bf16[32,768]{1,0:T(8,128)(2,1)}), bf16[1024,768]{1,0:T(8,128)(2,1)}) %all-gather.17.cloned.1.call-update) | async-done | bytes 1572880 | tf_op jit(solution)/shard_map/all_gather | solution.py:158
  384.7 94.7 %reduce-scatter.9.cloned.1.call-done = f32[32,768]{1,0:T(8,128)} async-done(((f32[1024,768]{1,0:T(8,128)}), f32[32,768]{1,0:T(8,128)}) %reduce-scatter.9.cloned.1.call-update) | async-done | bytes 98320 | tf_op jit(solution)/shard_map/reduce_scatter | solution.py:184
  491.6 11.6 multiply_reduce_fusion.2
  513.3 29.3 %convert_reduce_fusion.1 = (f32[3072]{0:T(1024)}, bf16[2048,3072]{1,0:T(8,128)(2,1)}) fusion(f32[2048,3072]{1,0:T(8,128)} %get-tuple-element.132, bf16[2048,768]{1,0:T(8,128)(2,1)S(1)} %get-tuple-element.118, bf16[3072,768]{1,0:T(8,128)(2,1)} %all-gather.13.cloned.1.call-done, f32[2048,3072]{1,0:T(8,128)} %get-tuple-element.147, ...), kind=kOutput, calls=%fused_computation.5 | convolution fusion | flops 9770628096 | bytes 70803456 | tf_op jit(solution)/shard_map/dot_general | solution.py:35
  542.6 19.7 %multiply_reduce_fusion.3 = (f32[768]{0:T(1024)}, f32[2048]{0:T(1024)S(1)}, f32[768]{0:T(1024)}, f32[2048,768]{1,0:T(8,128)S(1)}) fusion(f32[2048,768]{1,0:T(8,128)} %copy-done.2, f32[2048]{0:T(1024)S(1)} %fusion.38, f32[2048]{0:T(1024)S(1)} %broadcast_multiply_fusion.1, f32[768]{0:T(1024)S(1)} %convert_element_type.148, ...), kind=kOutput, calls=%fused_computation.50 | convolution fusion | flops 9679400960 | bytes 36217856 | tf_op jit(solution)/shard_map/dot_general | solution.py:35
  584.6 17.4 %multiply_reduce_fusion = (f32[64,12,32]{2,1,0:T(8,128)S(1)}, f32[64,12,32,32]{2,3,1,0:T(8,128)}) fusion(f32[64,12,32,32]{2,3,1,0:T(8,128)} %get-tuple-element.145, f32[64,12,32]{2,1,0:T(8,128)} %copy-done.16, bf16[64,32,1,12,64]{4,3,2,1,0:T(8,128)(2,1)} %get-tuple-element.137, bf16[64,32,12,64]{3,2,1,0:T(8,128)(2,1)} %reshape.281), kind=kOutput, calls=%fused_computation.25 | convolution fusion | flops 102998016 | bytes 12779520 | tf_op jit(solution)/shard_map/sqhe,skhe->shqk/dot_general | solution.py:231
  602.0 10.1 multiply_convert_fusion.1
  612.2 9.7 multiply_bitcast_fusion.1
  635.6 11.2 fusion.27
  646.9 12.6 %convert_reduce_fusion = (f32[3,12,64]{2,1,0:T(8,128)S(1)}, bf16[64,32,3,12,64]{4,1,3,0,2:T(8,128)(2,1)S(1)}) fusion(bf16[64,32,1,12,64]{4,1,3,0,2:T(8,128)(2,1)} %fusion.27, bf16[64,32,1,12,64]{4,1,3,0,2:T(8,128)(2,1)} %multiply_bitcast_fusion, bf16[64,32,1,12,64]{4,1,3,0,2:T(8,128)(2,1)} %multiply_bitcast_fusion.1), kind=kLoop, calls=%fused_computation.3 | loop fusion | flops 18872064 | bytes 18883584 | tf_op jit(solution)/shard_map/reduce_sum | solution.py:41
  659.5 13.1 %copy.68 = bf16[64,32,3,12,64]{4,3,2,1,0:T(8,128)(2,1)} copy(bf16[64,32,3,12,64]{4,1,3,0,2:T(8,128)(2,1)S(1)} %get-tuple-element.122) | data formatting | bytes 18874368 | tf_op jit(solution)/shard_map/convert_element_type | solution.py:248
  672.6 30.4 %convert_element_type.171 = bf16[2048,2304]{1,0:T(8,128)(2,1)} reshape(bf16[64,32,3,12,64]{4,3,2,1,0:T(8,128)(2,1)} %copy.68) | data formatting | bytes 18874368 | tf_op jit(solution)/shard_map/convert_element_type | solution.py:248
  703.1 12.0 %convolution_bitcast_fusion = f32[768,2304]{0,1:T(8,128)} fusion(bf16[2048,2304]{1,0:T(8,128)(2,1)} %convert_element_type.171, bf16[2048,768]{1,0:T(8,128)(2,1)S(1)} %bitcast.109), kind=kOutput, calls=%fused_computation.69 | convolution fusion | flops 7247757312 | bytes 19660800 | tf_op jit(solution)/shard_map/dot_general | solution.py:29
  723.2 16.2 %fusion.64 = f32[3072,768]{1,0:T(8,128)} fusion(bf16[2048,3072]{1,0:T(8,128)(2,1)} %get-tuple-element.131, bf16[2048,768]{1,0:T(8,128)(2,1)} %copy-done.12), kind=kOutput, calls=%fused_computation.141 | convolution fusion | flops 9663676416 | bytes 25165824 | tf_op jit(solution)/shard_map/dot_general | solution.py:29
  740.1 18.4 %fusion.44 = f32[768,3072]{1,0:T(8,128)} fusion(bf16[2048,3072]{1,0:T(8,128)(2,1)} %get-tuple-element.157, f32[2048,768]{1,0:T(8,128)} %copy-done.2, f32[768]{0:T(1024)S(1)} %copy-done.36, f32[768]{0:T(1024)S(1)} %convert_element_type.148, f32[2048]{0:T(1024)S(1)} %fusion.38, f32[2048]{0:T(1024)S(1)} %broadcast_multiply_fusion.1), kind=kOutput, calls=%fused_computation.128 | convolution fusion | flops 9671540736 | bytes 28334080 | tf_op jit(solution)/shard_map/dot_general | solution.py:29
  768.2 41.0 %all-reduce.18 = (f32[]{:T(128)}, f32[4]{0:T(128)S(1)}, f32[1536]{0:T(1024)S(1)}, f32[768]{0:T(1024)S(1)}, f32[768]{0:T(1024)S(1)}, /*index=5*/f32[768]{0:T(1024...) all-reduce(f32[]{:T(128)} %get-tuple-element.127, ...), channel_id=1, replica_groups=mesh['fsdp'=8,'dp'=4] {'fsdp','dp'}, use_global_device_ids=true, to_apply=%region_11.12 | all-reduce | flops 9989 | bytes 79912 | tf_op jit(solution)/shard_map/psum | solution.py:177
  816.9 13.6 %add_convert_fusion.2 = bf16[2048,768]{1,0:T(8,128)(2,1)} fusion(f32[2048,768]{1,0:T(8,128)} %copy-done.4, bf16[2048,2304]{1,0:T(8,128)(2,1)} %convert_element_type.171, bf16[768,2304]{1,0:T(8,128)(2,1)} %all-gather.7.cloned.1.call-done, f32[2048]{0:T(1024)S(1)} %copy-done.25), kind=kOutput, calls=%fused_computation.52 | convolution fusion | flops 7252475904 | bytes 22421504 | tf_op jit(solution)/shard_map/dot_general | solution.py:35
  830.5 39.3 %reduce-scatter.19.cloned.1.call-done = f32[24,2304]{1,0:T(8,128)} async-done(((f32[768,2304]{1,0:T(8,128)}), f32[24,2304]{1,0:T(8,128)}) %reduce-scatter.19.cloned.1.call-update) | async-done | bytes 221200
  869.8 142.3 %reduce-scatter.15.cloned.1.call-done = f32[96,768]{1,0:T(8,128)} async-done(((f32[3072,768]{1,0:T(8,128)}), f32[96,768]{1,0:T(8,128)}) %reduce-scatter.15.cloned.1.call-update) | async-done | bytes 294928 | tf_op jit(solution)/shard_map/reduce_scatter | solution.py:211
  1012.1 141.0 %reduce-scatter.13.cloned.1.call-done = f32[24,3072]{1,0:T(8,128)} async-done(((f32[768,3072]{1,0:T(8,128)}), f32[24,3072]{1,0:T(8,128)}) %reduce-scatter.13.cloned.1.call-update) | async-done | bytes 294928 | tf_op jit(solution)/shard_map/reduce_scatter | solution.py:209
  (208 shorter events, 140.1 us)
Async XLA Ops:
  7.2 71.1 %all-gather.7.cloned.1.call-start = ((), (), s32[]{:S(2)}) async-start(), calls=%async_computation.6 | async-start | bytes 3649536 | tf_op jit(solution)/shard_map/all_gather | solution.py:72
  7.9 192.5 %all-gather.9.cloned.1.call-start = ((), (), s32[]{:S(2)}) async-start(), calls=%async_computation.7 | async-start | bytes 1216512 | tf_op jit(solution)/shard_map/all_gather | solution.py:74
  8.7 206.0 %all-gather.11.cloned.1.call-start = ((), (), s32[]{:S(2)}) async-start(), calls=%async_computation.8 | async-start | bytes 4866048 | tf_op jit(solution)/shard_map/all_gather | solution.py:125
  9.4 275.5 %all-gather.13.cloned.1.call-start = ((), (), s32[]{:S(2)}) async-start(), calls=%async_computation.9 | async-start | bytes 4866048 | tf_op jit(solution)/shard_map/all_gather | solution.py:127
  10.0 306.0 %all-gather.15.cloned.1.call-start = ((), (), s32[]{:S(2)}) async-start(), calls=%async_computation.10 | async-start | bytes 1216512 | tf_op jit(solution)/shard_map/all_gather | solution.py:131
  10.6 362.7 %all-gather.17.cloned.1.call-start = ((), (), s32[]{:S(2)}) async-start(), calls=%async_computation.11 | async-start | bytes 1622016 | tf_op jit(solution)/shard_map/all_gather | solution.py:158
  61.5 15.5 %copy-start.18 = (f32[32,32]{1,0:T(8,128)}, f32[32,32]{1,0:T(8,128)S(1)}, u32[]{:S(2)}) copy-start(f32[32,32]{1,0:T(8,128)S(1)} %get-tuple-element.142) | copy-start | bytes 12292
  68.2 216.6 %copy-start.35 = (f32[768]{0:T(1024)}, f32[768]{0:T(1024)S(1)}, u32[]{:S(2)}) copy-start(f32[768]{0:T(1024)S(1)} %convert_element_type.149) | copy-start | bytes 9220
  68.8 9.5 copy-start.6
  166.1 11.4 copy-start.16
  214.7 70.2 %copy-start.37 = (f32[768]{0:T(1024)S(1)}, f32[768]{0:T(1024)}, u32[]{:S(2)}) copy-start(f32[768]{0:T(1024)} %convert_element_type.153) | copy-start | bytes 9220
  305.4 10.6 copy-start.28
  318.5 160.9 %reduce-scatter.9.cloned.1.call-start = ((), (), s32[]{:S(2)}) async-start(), calls=%async_computation.12 | async-start | bytes 3244032 | tf_op jit(solution)/shard_map/reduce_scatter | solution.py:184
  378.7 105.4 %copy-start.10 = (bf16[768,768]{1,0:T(8,128)(2,1)S(1)}, bf16[768,768]{1,0:T(8,128)(2,1)}, u32[]{:S(2)}) copy-start(bf16[768,768]{1,0:T(8,128)(2,1)} %all-gather.15.cloned.1.call-done) | copy-start | bytes 3538948
  378.7 451.8 %reduce-scatter.17.cloned.1.call-start = ((), (), s32[]{:S(2)}) async-start(), calls=%async_computation.16 | async-start | bytes 2433024 | tf_op jit(solution)/shard_map/reduce_scatter | solution.py:215
  484.0 346.5 %reduce-scatter.11.cloned.1.call-start = ((), (), s32[]{:S(2)}) async-start(), calls=%async_computation.13 | async-start | bytes 2433024 | tf_op jit(solution)/shard_map/reduce_scatter | solution.py:264
  484.6 18.6 %slice-start = ((s8[6291456]{0:T(1024)(128)(4,1)}), s8[2097152]{0:T(1024)(128)(4,1)S(1)}, s32[]{:S(2)}) async-start(s8[6291456]{0:T(1024)(128)(4,1)} %bitcast.106), calls=%async_computation.18 | async-start | bytes 4194304
  491.6 11.6 copy-start
  491.6 11.7 %slice-start.1 = ((s8[6291456]{0:T(1024)(128)(4,1)}), s8[4194304]{0:T(1024)(128)(4,1)S(1)}, s32[]{:S(2)}) async-start(s8[6291456]{0:T(1024)(128)(4,1)} %bitcast.106), calls=%async_computation.19 | async-start | bytes 8388608
  513.3 29.3 %copy-start.12 = (bf16[2048,768]{1,0:T(8,128)(2,1)}, bf16[2048,768]{1,0:T(8,128)(2,1)S(1)}, u32[]{:S(2)}) copy-start(bf16[2048,768]{1,0:T(8,128)(2,1)S(1)} %get-tuple-element.118) | copy-start | bytes 9437188
  542.6 19.7 %copy-start.22 = (f32[2048]{0:T(1024)S(1)}, f32[2048]{0:T(1024)}, u32[]{:S(2)}) copy-start(f32[2048]{0:T(1024)} %copy-done.21) | copy-start | bytes 24580
  584.6 17.4 %copy-start.17 = (f32[64,12,32]{2,1,0:T(8,128)S(1)}, f32[64,12,32]{2,1,0:T(8,128)}, u32[]{:S(2)}) copy-start(f32[64,12,32]{2,1,0:T(8,128)} %copy-done.16) | copy-start | bytes 294916
  612.2 9.7 copy-start.3
  612.2 9.7 copy-start.8
  612.2 9.7 copy-start.14
  646.9 222.9 %reduce-scatter.19.cloned.1.call-start = ((), (), s32[]{:S(2)}) async-start(), calls=%async_computation.17 | async-start | bytes 7299072
  672.6 30.4 %copy-start.7 = (bf16[2,32,32,768]{3,2,1,0:T(8,128)(2,1)S(1)}, bf16[2,32,32,768]{3,2,1,0:T(8,128)(2,1)}, u32[]{:S(2)}) copy-start(bf16[2,32,32,768]{3,2,1,0:T(8,128)(2,1)} %param.21) | copy-start | bytes 9437188
  723.1 288.9 %reduce-scatter.15.cloned.1.call-start = ((), (), s32[]{:S(2)}) async-start(), calls=%async_computation.15 | async-start | bytes 9732096 | tf_op jit(solution)/shard_map/reduce_scatter | solution.py:211
  739.4 413.6 %reduce-scatter.13.cloned.1.call-start = ((), (), s32[]{:S(2)}) async-start(), calls=%async_computation.14 | async-start | bytes 9732096 | tf_op jit(solution)/shard_map/reduce_scatter | solution.py:209
  759.2 9.0 copy-start.32
  759.2 9.0 copy-start.33
  759.2 57.7 %copy-start.25 = (f32[2048]{0:T(1024)S(1)}, f32[2048]{0:T(1024)}, u32[]{:S(2)}) copy-start(f32[2048]{0:T(1024)} %copy-done.24) | copy-start | bytes 24580
  (21 other events, 93.1 us)
Sparse Core Ops, SparseCore 0:
  10.9 63.0 all-gather.6
  76.9 52.8 all-gather.8
  132.7 62.4 all-gather.10
  198.0 62.3 all-gather.12
  263.1 52.8 all-gather.14
  319.3 53.9 all-gather.16
  378.8 100.5 reduce-scatter.8
  485.2 97.9 reduce-scatter.16
  647.0 97.9 reduce-scatter.10
  751.1 118.6 reduce-scatter.18
  877.3 134.7 reduce-scatter.14
  1018.4 134.5 reduce-scatter.12
where the time goes:
time: 1170 us; the launch traced here: 1160 us
  waiting for transfers between devices  482 us (41%)
  matrix products  310 us (26%)
  local copies, waits for them, and re-layouts  156 us (13%)
  other arithmetic  111 us (9%)
  blocking collectives  83.6 us (7%)
  between operations  18.3 us (2%)
    reduce_scatter x1, waiting for transfers between devices, on_device(): lax.psum_scatter(grad_narrow_weight, ('fsdp', 'dp'), scatter_dimension=0,...  142 us
    reduce_scatter x1, waiting for transfers between devices, on_device(): lax.psum_scatter(grad_widen_weight, ('fsdp', 'dp'), scatter_dimension=0,...  141 us
    reduce_scatter x1, waiting for transfers between devices, on_device(): lax.psum_scatter(dsecond_all, ('fsdp', 'dp'), scatter_dimension=0, tiled=...  94.7 us
    dot_general x1, matrix products, on_device(): jnp.dot(hidden_low, widen, preferred_element_type=jnp.float32)  70.2 us
    dot_general x6, matrix products, times_transpose(): lax.dot_general(left_side, right_side, (((1,), (1,)), ((), ())), preferre...  68 us
    dot_general x6, matrix products, rows_product(): lax.dot_general(left_side, right_side, (((0,), (0,)), ((), ())), preferre...  55.1 us
    all_gather x1, waiting for transfers between devices, on_device(): lax.all_gather(second_unit, ('fsdp', 'dp'), axis=0, tiled=True)  54.8 us
    convert_element_type x2, local copies, waits for them, and re-layouts, on_device(): dpacked = jnp.stack([dqueries, dkey_rows, dvalues], axis=2).astype(jnp.bf...  43.5 us
  transfers between devices with their start and end apart: 12, of which 6 were waited for; matrix products, arithmetic and copies ran while one was open for 48% of the time, Pallas kernels for 0%

commit v1 on v0

v1 whole, which is shorter than its diff:
```python
import functools

import jax
import jax.numpy as jnp
from jax import lax
from jax.experimental import pallas as pl
from jax.experimental.pallas import tpu as pltpu
from jax.sharding import PartitionSpec as P

HEADS = 12
DROP_SCALE = 1.0 / 0.9
SOFTMAX_TEMP = 0.05
INV_TEMP = 20.0
AXES = ("fsdp", "dp")
F32 = jnp.float32
BF16 = jnp.bfloat16
LANES = 128
MASKED = -1e30
ROWS = 256
SUB = 128
VMEM_LIMIT = 60 * 1024 * 1024
ROOT_HALF = 0.7071067811865476
INV_ROOT_TAU = 0.3989422804014327


def dot(a, b):
    return jnp.dot(a, b, preferred_element_type=F32)


def dot_nt(a, b):
    return lax.dot_general(a, b, (((1,), (1,)), ((), ())), preferred_element_type=F32)


def dot_tn(a, b):
    return lax.dot_general(a, b, (((0,), (0,)), ((), ())), preferred_element_type=F32)


def iota(shape, dim):
    return lax.broadcasted_iota(jnp.int32, shape, dim)


def head_masks():
    lane = iota((1, LANES), 1)
    return lane < 64, lane >= 64


def two_heads(rows, scale):
    low, high = head_masks()
    s = jnp.asarray(scale, BF16)
    zero = jnp.zeros_like(rows)
    scaled = rows * s if scale != 1.0 else rows
    return jnp.concatenate([jnp.where(low, scaled, zero), jnp.where(high, scaled, zero)], axis=0)


def lane_lengths(lens_ref, first, count, group, shape, dim):
    where = iota(shape, dim) // group
    out = jnp.zeros(shape, jnp.int32)
    for k in range(count):
        out = jnp.where(where == k, lens_ref[first + k], out)
    return out


def row_valid(lens_ref, step, rows, length):
    per = rows // length
    first = lax.rem(step * per, lens_ref.shape[0])
    shape = (rows, LANES)
    lens = lane_lengths(lens_ref, first, per, length, shape, 0)
    return (iota(shape, 0) % length < lens).astype(F32)


def masked_square(values, valid):
    total = None
    for c in range(values.shape[1] // LANES):
        part = values[:, c * LANES : (c + 1) * LANES]
        part = part * part * valid
        total = part if total is None else total + part
    return jnp.sum(total.reshape(-1, 8, LANES), axis=0)


def normalise(values):
    centred = values - jnp.mean(values, axis=-1, keepdims=True)
    rho = lax.rsqrt(jnp.mean(centred * centred, axis=-1, keepdims=True) + 1e-12)
    return centred * rho, rho


def norm_back(dout, c, rho, gain):
    dg = dout * gain
    return rho * (
        dg - jnp.mean(dg, axis=-1, keepdims=True) - c * jnp.mean(dg * c, axis=-1, keepdims=True)
    )


def attn_fwd_kernel(
    lens_ref, x_ref, drop_ref, w_ref, wb_ref, m_ref, mb_ref,
    packed_ref, p_ref, ctx_ref, c_ref, rho_ref, first_ref, sums_ref,
    *, length,
):
    step = pl.program_id(0)
    x = x_ref[...]
    width = x.shape[1]
    for t in range(3):
        cols = slice(t * width, (t + 1) * width)
        packed_ref[:, cols] = (dot(x, w_ref[:, cols]) + wb_ref[:, cols]).astype(BF16)
    per = SUB // length
    for u in range(ROWS // SUB):
        rows = slice(u * SUB, (u + 1) * SUB)
        first = lax.rem(step * (ROWS // length) + u * per, lens_ref.shape[0])
        shape = (SUB, SUB)
        lens = lane_lengths(lens_ref, first, per, length, shape, 1)
        lane = iota(shape, 1)
        seen = (iota(shape, 0) // length == lane // length) & (lane % length < lens)
        bias = jnp.where(seen, 0.0, MASKED).astype(F32)
        for pair in range(width // LANES):
            a = pair * LANES
            q = packed_ref[rows, a : a + LANES]
            k = packed_ref[rows, width + a : width + a + LANES]
            v = packed_ref[rows, 2 * width + a : 2 * width + a + LANES]
            scores = dot_nt(q, two_heads(k, 0.125))
            halves = []
            for h in range(2):
                s = scores[:, h * SUB : (h + 1) * SUB] + bias
                e = jnp.exp(s - jnp.max(s, axis=-1, keepdims=True))
                halves.append((e * (1.0 / jnp.sum(e, axis=-1, keepdims=True))).astype(BF16))
            p = jnp.concatenate(halves, axis=1)
            p_ref[rows, pair * 2 * SUB : (pair + 1) * 2 * SUB] = p
            ctx_ref[rows, a : a + LANES] = dot(p, two_heads(v, 1.0)).astype(BF16)
    branch = dot(ctx_ref[...], m_ref[...]) + mb_ref[...]
    part = branch * (drop_ref[...].astype(F32) * DROP_SCALE)
    xf = x.astype(F32)
    valid = row_valid(lens_ref, step, ROWS, length)
    sums_ref[0, 0] = masked_square(xf, valid)
    sums_ref[0, 1] = masked_square(part, valid)
    c, rho = normalise(xf + part)
    c_ref[...] = c
    rho_ref[...] = rho
    first_ref[...] = jnp.concatenate(
        [c[k * length : k * length + 1] for k in range(ROWS // length)], axis=0
    )


def resident(shape, column=0):
    return pl.BlockSpec(shape, lambda *_: (0, column), pipeline_mode=pl.Buffered(1))


MIXER, POOLER = 4, 5


def row_block(cols, rows=ROWS):
    return pl.BlockSpec((rows, cols), lambda i, *_: (i, 0))


def params():
    return pltpu.CompilerParams(vmem_limit_bytes=VMEM_LIMIT)


def attn_fwd(lens, x, drop, weights, wb, mixer, mb, length):
    n, d = x.shape
    steps = n // ROWS
    per = ROWS // length
    f = lambda cols, t, rows=n: jax.ShapeDtypeStruct((rows, cols), t)
    return pl.pallas_call(
        functools.partial(attn_fwd_kernel, length=length),
        name="attn_fwd",
        grid_spec=pltpu.PrefetchScalarGridSpec(
            num_scalar_prefetch=1,
            grid=(steps,),
            in_specs=[
                row_block(d), row_block(d),
                resident((d, 3 * d)), resident((1, 3 * d)), resident((d, d), MIXER), resident((1, d)),
            ],
            out_specs=[
                row_block(3 * d), row_block(2 * d), row_block(d), row_block(d), row_block(1),
                row_block(d, per), pl.BlockSpec((1, 2, 8, LANES), lambda i, *_: (i, 0, 0, 0)),
            ],
        ),
        out_shape=[
            f(3 * d, BF16), f(2 * d, BF16), f(d, BF16), f(d, F32), f(1, F32),
            f(d, F32, steps * per), jax.ShapeDtypeStruct((steps, 2, 8, LANES), F32),
        ],
        compiler_params=params(),
        cost_estimate=pl.CostEstimate(
            flops=2 * n * d * d * 6, bytes_accessed=n * d * 26, transcendentals=n * d
        ),
    )(lens, x, drop, weights, wb, mixer, mb)


CHUNK = 512


def ffn_chunk(hl, ww_ref, wwb_ref, cols):
    u = dot(hl, ww_ref[:, cols]) + wwb_ref[:, cols]
    phi = 0.5 + 0.5 * lax.erf(u * ROOT_HALF)
    return u, phi


def ffn_fwd_kernel(
    lens_ref, c_ref, drop_ref, g1_ref, s1_ref, ww_ref, wwb_ref, wn_ref, wnb_ref, g2_ref, s2_ref,
    hl_ref, act_ref, slope_ref, c2_ref, rho_ref, out_ref, sums_ref,
    *, length,
):
    step = pl.program_id(0)
    hidden = c_ref[...] * g1_ref[...] + s1_ref[...]
    hl = hidden.astype(BF16)
    hl_ref[...] = hl
    total = None
    for ch in range(ww_ref.shape[1] // CHUNK):
        cols = slice(ch * CHUNK, (ch + 1) * CHUNK)
        u, phi = ffn_chunk(hl, ww_ref, wwb_ref, cols)
        act = (u * phi).astype(BF16)
        act_ref[:, cols] = act
        slope_ref[:, cols] = (phi + u * (jnp.exp(u * u * -0.5) * INV_ROOT_TAU)).astype(BF16)
        part = dot(act, wn_ref[cols, :])
        total = part if total is None else total + part
    part = (total + wnb_ref[...]) * (drop_ref[...].astype(F32) * DROP_SCALE)
    valid = row_valid(lens_ref, step, ROWS, length)
    sums_ref[0] = masked_square(part, valid)
    c2, rho = normalise(hidden + part)
    c2_ref[...] = c2
    rho_ref[...] = rho
    normed = c2 * g2_ref[...] + s2_ref[...]
    out_ref[...] = (normed * valid[:, :1]).astype(BF16)


def ffn_fwd(lens, c, drop, g1, s1, ww, wwb, wn, wnb, g2, s2, length):
    n, d = c.shape
    ff = wn.shape[0]
    steps = n // ROWS
    f = lambda cols, t, rows=n: jax.ShapeDtypeStruct((rows, cols), t)
    return pl.pallas_call(
        functools.partial(ffn_fwd_kernel, length=length),
        name="ffn_fwd",
        grid_spec=pltpu.PrefetchScalarGridSpec(
            num_scalar_prefetch=1,
            grid=(steps,),
            in_specs=[
                row_block(d), row_block(d), resident((1, d)), resident((1, d)),
                resident((d, ff)), resident((1, ff)), resident((ff, d)), resident((1, d)),
                resident((1, d)), resident((1, d)),
            ],
            out_specs=[
                row_block(d), row_block(ff), row_block(ff), row_block(d), row_block(1),
                row_block(d), pl.BlockSpec((1, 8, LANES), lambda i, *_: (i, 0, 0)),
            ],
        ),
        out_shape=[
            f(d, BF16), f(ff, BF16), f(ff, BF16), f(d, F32), f(1, F32), f(d, BF16),
            jax.ShapeDtypeStruct((steps, 8, LANES), F32),
        ],
        compiler_params=params(),
        cost_estimate=pl.CostEstimate(
            flops=4 * n * d * ff, bytes_accessed=n * d * 32, transcendentals=2 * n * ff
        ),
    )(lens, c, drop, g1, s1, ww, wwb, wn, wnb, g2, s2)


def first_kernel(
    c_ref, drop_ref, g1_ref, s1_ref, ww_ref, wwb_ref, wn_ref, wnb_ref, g2_ref, s2_ref,
    wp_ref, wpb_ref, unit_ref, pooled_ref, rho_ref, first_ref,
):
    hidden = c_ref[...] * g1_ref[...] + s1_ref[...]
    hl = hidden.astype(BF16)
    total = None
    for ch in range(ww_ref.shape[1] // CHUNK):
        cols = slice(ch * CHUNK, (ch + 1) * CHUNK)
        u, phi = ffn_chunk(hl, ww_ref, wwb_ref, cols)
        part = dot((u * phi).astype(BF16), wn_ref[cols, :])
        total = part if total is None else total + part
    part = (total + wnb_ref[...]) * (drop_ref[...].astype(F32) * DROP_SCALE)
    c2, _ = normalise(hidden + part)
    first = (c2 * g2_ref[...] + s2_ref[...]).astype(BF16)
    first_ref[...] = first
    pooled = jnp.tanh(dot(first, wp_ref[...]) + wpb_ref[...])
    rho = lax.rsqrt(jnp.sum(pooled * pooled, axis=-1, keepdims=True) + 1e-6)
    pooled_ref[...] = pooled
    rho_ref[...] = rho
    unit_ref[...] = (pooled * rho).astype(BF16)


def first_tokens(c, drop, g1, s1, ww, wwb, wn, wnb, g2, s2, wpb):
    n, d = c.shape
    ff = wn.shape[0]
    vector = resident((1, d))
    f = lambda cols, t: jax.ShapeDtypeStruct((n, cols), t)
    return pl.pallas_call(
        first_kernel,
        name="first_tokens",
        grid=(1,),
        in_specs=[
            resident((n, d)), resident((n, d)), vector, vector, resident((d, ff)), resident((1, ff)),
            resident((ff, d)), vector, vector, vector, resident((d, d), POOLER), vector,
        ],
        out_specs=[resident((n, d)), resident((n, d)), resident((n, 1)), resident((n, d))],
        out_shape=[f(d, BF16), f(d, F32), f(1, F32), f(d, BF16)],
        compiler_params=params(),
    )(c, drop, g1, s1, ww, wwb, wn, wnb, g2, s2, ww, wpb)


def loss_kernel(
    place_ref, one_ref, two_ref, pooled_ref, rho_ref, first_ref, wp_ref,
    loss_ref, dfirst_ref, gw_ref, gb_ref,
):
    total = one_ref.shape[0]
    mine = pooled_ref.shape[0] // 2
    start = pl.multiple_of(place_ref[0] * mine, mine)
    block = 256
    logs, worth = [], jnp.zeros((1, 1), F32)
    for b in range(total // block):
        rows = one_ref[b * block : (b + 1) * block, :]
        similar = dot_nt(two_ref[...], rows)
        log_total = jnp.log(jnp.sum(jnp.exp(similar * INV_TEMP), axis=0, keepdims=True))
        same = iota(similar.shape, 0) == iota(similar.shape, 1) + b * block
        positive = jnp.sum(jnp.where(same, similar, 0.0), axis=0, keepdims=True)
        logs.append(log_total)
        worth = worth + jnp.sum(log_total - positive * INV_TEMP, axis=1, keepdims=True)
    loss_ref[...] = worth * (1.0 / total)
    log_total = jnp.concatenate(logs, axis=1)
    shape = (mine, total)
    same = (iota(shape, 0) + start == iota(shape, 1)).astype(F32)
    similar = dot_nt(two_ref[pl.ds(start, mine), :], one_ref[...])
    dsim = ((jnp.exp(similar * INV_TEMP - log_total) - same) * INV_TEMP).astype(BF16)
    dtwo = dot(dsim, one_ref[...])
    similar = dot_nt(one_ref[pl.ds(start, mine), :], two_ref[...]) * INV_TEMP
    own = jnp.log(jnp.sum(jnp.exp(similar), axis=1, keepdims=True))
    dsim = ((jnp.exp(similar - own) - same) * INV_TEMP).astype(BF16)
    done = dot(dsim, two_ref[...])
    dunit = jnp.concatenate([done, dtwo], axis=0)
    pooled, rho = pooled_ref[...], rho_ref[...]
    inner = jnp.sum(pooled * dunit, axis=-1, keepdims=True)
    dpool = ((1.0 - pooled * pooled) * (rho * dunit - rho * rho * rho * pooled * inner)).astype(BF16)
    dfirst_ref[...] = dot_nt(dpool, wp_ref[...])
    gw_ref[...] = dot_tn(first_ref[...], dpool)
    gb_ref[...] = jnp.sum(dpool.astype(F32), axis=0, keepdims=True)


def loss_parts(place, one, two, pooled, rho, first, wp):
    n, d = pooled.shape
    f = lambda r, c: jax.ShapeDtypeStruct((r, c), F32)
    whole = [one, two, pooled, rho, first]
    return pl.pallas_call(
        loss_kernel,
        name="loss",
        grid=(1,),
        in_specs=[pl.BlockSpec(memory_space=pltpu.SMEM)]
        + [resident(v.shape) for v in whole]
        + [resident((d, d), POOLER)],
        out_specs=[resident((1, 1)), resident((n, d)), resident((d, d)), resident((1, d))],
        out_shape=[f(1, 1), f(n, d), f(d, d), f(1, d)],
        compiler_params=params(),
    )(place, one, two, pooled, rho, first, wp)


def ffn_back_kernel(
    lens_ref, cot_ref, dfirst_ref, c2_ref, rho2_ref, drop2_ref, slope_ref, c_ref, rho_ref, drop_ref,
    g1_ref, ww_ref, wn_ref, g2_ref,
    dnarrow_ref, dwide_ref, dres_ref, dbranch_ref, rows_ref, wide_ref,
    *, length,
):
    step = pl.program_id(0)
    d = c_ref.shape[1]

    @pl.when(step == 0)
    def _():
        rows_ref[...] = jnp.zeros_like(rows_ref)
        wide_ref[...] = jnp.zeros_like(wide_ref)

    def add_row(k, values):
        rows_ref[k : k + 1, :] += jnp.sum(values, axis=0, keepdims=True)

    valid = row_valid(lens_ref, step, ROWS, length)[:, :1]
    per = ROWS // length
    dout = cot_ref[...].astype(F32).reshape(per, length, d)
    is_first = iota((per, length, d), 1) == 0
    dout = dout + jnp.where(is_first, dfirst_ref[...][:, None, :], 0.0)
    dout = dout.reshape(ROWS, d) * valid
    c2 = c2_ref[...]
    add_row(0, dout * c2)
    add_row(1, dout)
    dsecond = norm_back(dout, c2, rho2_ref[...], g2_ref[...])
    dnarrow = (dsecond * (drop2_ref[...].astype(F32) * DROP_SCALE)).astype(BF16)
    dnarrow_ref[...] = dnarrow
    add_row(2, dnarrow.astype(F32))
    dhidden = dsecond
    for ch in range(ww_ref.shape[1] // CHUNK):
        cols = slice(ch * CHUNK, (ch + 1) * CHUNK)
        dactive = dot_nt(dnarrow, wn_ref[cols, :])
        dwide = (dactive * slope_ref[:, cols].astype(F32)).astype(BF16)
        dwide_ref[:, cols] = dwide
        wide_ref[0:1, cols] += jnp.sum(dwide.astype(F32), axis=0, keepdims=True)
        dhidden = dhidden + dot_nt(dwide, ww_ref[:, cols])
    c = c_ref[...]
    add_row(3, dhidden * c)
    add_row(4, dhidden)
    dres = norm_back(dhidden, c, rho_ref[...], g1_ref[...])
    dres_ref[...] = dres
    dbranch = (dres * (drop_ref[...].astype(F32) * DROP_SCALE)).astype(BF16)
    dbranch_ref[...] = dbranch
    add_row(5, dbranch.astype(F32))


def ffn_back(lens, cot, dfirst, c2, rho2, drop2, slope, c, rho, drop, g1, ww, wn, g2, length):
    n, d = c.shape
    ff = wn.shape[0]
    steps = n // ROWS
    f = lambda cols, t, rows=n: jax.ShapeDtypeStruct((rows, cols), t)
    whole = lambda r, c: pl.BlockSpec((r, c), lambda i, *_: (0, 0))
    return pl.pallas_call(
        functools.partial(ffn_back_kernel, length=length),
        name="ffn_back",
        grid_spec=pltpu.PrefetchScalarGridSpec(
            num_scalar_prefetch=1,
            grid=(steps,),
            in_specs=[
                row_block(d), row_block(d, ROWS // length), row_block(d), row_block(1),
                row_block(d), row_block(ff), row_block(d), row_block(1), row_block(d),
                resident((1, d)), resident((d, ff)), resident((ff, d)), resident((1, d)),
            ],
            out_specs=[
                row_block(d), row_block(ff), row_block(d), row_block(d), whole(8, d), whole(8, ff),
            ],
        ),
        out_shape=[f(d, BF16), f(ff, BF16), f(d, F32), f(d, BF16), f(d, F32, 8), f(ff, F32, 8)],
        compiler_params=params(),
        cost_estimate=pl.CostEstimate(
            flops=4 * n * d * ff, bytes_accessed=n * d * 40, transcendentals=0
        ),
    )(lens, cot, dfirst, c2, rho2, drop2, slope, c, rho, drop, g1, ww, wn, g2)


def attn_back_kernel(
    dbranch_ref, dres_ref, packed_ref, p_ref, w_ref, m_ref, dpacked_ref, dx_ref, rows_ref
):
    step = pl.program_id(0)
    width = dres_ref.shape[1]

    @pl.when(step == 0)
    def _():
        rows_ref[...] = jnp.zeros_like(rows_ref)

    low, _ = head_masks()
    dctx = dot_nt(dbranch_ref[...], m_ref[...]).astype(BF16)
    for u in range(ROWS // SUB):
        rows = slice(u * SUB, (u + 1) * SUB)
        for pair in range(width // LANES):
            a = pair * LANES
            q = packed_ref[rows, a : a + LANES]
            k2 = two_heads(packed_ref[rows, width + a : width + a + LANES], 0.125)
            v2 = two_heads(packed_ref[rows, 2 * width + a : 2 * width + a + LANES], 1.0)
            p = p_ref[rows, pair * 2 * SUB : (pair + 1) * 2 * SUB]
            dc = dctx[rows, a : a + LANES]
            dp = dot_nt(dc, v2)
            pf = p.astype(F32)
            parts = []
            for h in range(2):
                cols = slice(h * SUB, (h + 1) * SUB)
                t = pf[:, cols] * dp[:, cols]
                parts.append((t - pf[:, cols] * jnp.sum(t, axis=-1, keepdims=True)).astype(BF16))
            ds = jnp.concatenate(parts, axis=1)
            dpacked_ref[rows, a : a + LANES] = dot(ds, k2).astype(BF16)
            dk = dot_tn(ds, q)
            dk = jnp.where(low, dk[:SUB], dk[SUB:]) * 0.125
            dpacked_ref[rows, width + a : width + a + LANES] = dk.astype(BF16)
            dv = dot_tn(p, dc)
            dv = jnp.where(low, dv[:SUB], dv[SUB:])
            dpacked_ref[rows, 2 * width + a : 2 * width + a + LANES] = dv.astype(BF16)
    total = dres_ref[...]
    for t in range(3):
        cols = slice(t * width, (t + 1) * width)
        part = dpacked_ref[:, cols]
        rows_ref[0:1, cols] += jnp.sum(part.astype(F32), axis=0, keepdims=True)
        total = total + dot_nt(part, w_ref[:, cols])
    dx_ref[...] = total.astype(BF16)


def attn_back(dbranch, dres, packed, p, weights, mixer):
    n, d = dres.shape
    f = lambda cols, t, rows=n: jax.ShapeDtypeStruct((rows, cols), t)
    return pl.pallas_call(
        attn_back_kernel,
        name="attn_back",
        grid=(n // ROWS,),
        in_specs=[
            row_block(d), row_block(d), row_block(3 * d), row_block(2 * d),
            resident((d, 3 * d)), resident((d, d), MIXER),
        ],
        out_specs=[row_block(3 * d), row_block(d), pl.BlockSpec((8, 3 * d), lambda i: (0, 0))],
        out_shape=[f(3 * d, BF16), f(d, BF16), f(3 * d, F32, 8)],
        compiler_params=params(),
        cost_estimate=pl.CostEstimate(
            flops=2 * n * d * d * 8, bytes_accessed=n * d * 24, transcendentals=0
        ),
    )(dbranch, dres, packed, p, weights, mixer)


class Links:
    def __init__(self):
        self.fsdp, self.dp = lax.axis_size("fsdp"), lax.axis_size("dp")
        self.depth = self.fsdp // 2
        f, g = lax.axis_index("fsdp"), lax.axis_index("dp")
        self.place = (f * self.dp + g).astype(jnp.int32).reshape(1)
        self.coords = jnp.stack([f // 2, f % 2, g // 2, g % 2]).astype(jnp.int32)

    def square(self):
        return self.dp == 4 and self.depth == 4

    def send(self, value, core=0, a=0, b=0, z=0):
        pairs = []
        for i in range(self.fsdp * self.dp):
            f, g = divmod(i, self.dp)
            to_f = (f // 2 + z) % self.depth * 2 + (f % 2 ^ core)
            to_g = (g // 2 ^ a) * 2 + (g % 2 ^ b)
            pairs.append((i, to_f * self.dp + to_g))
        return lax.ppermute(value, AXES, pairs)


def owner(coords_ref, z, core, a, b):
    zz = lax.rem(coords_ref[0] + (4 - z), 4)
    cc = lax.rem(coords_ref[1] + core, 2)
    aa = lax.rem(coords_ref[2] + a, 2)
    bb = lax.rem(coords_ref[3] + b, 2)
    return (zz * 2 + cc) * 4 + aa * 2 + bb


def spread_small(links, block):
    own = jnp.stack([block] + [links.send(block, z=k) for k in (1, 2, 3)])
    parts = [(own, 0, 0)] + [(links.send(own, a=a, b=b), a, b) for a, b in ((0, 1), (1, 0), (1, 1))]
    pieces = []
    for value, a, b in parts:
        for core, v in ((0, value), (1, links.send(value, core=1))):
            pieces.append((v, [((k,), k, core, a, b) for k in range(4)]))
    return pieces


def spread_first(links, block):
    return [block] + [links.send(block, z=k) for k in (1, 2, 3)]


def spread_large(links, along):
    left, right = jnp.stack(along[:2]), jnp.stack(along[2:])
    left = jnp.stack([left, links.send(left, b=1)])
    right = jnp.stack([right, links.send(right, a=1)])
    parts = [
        (left, lambda i, k: (k, 0, i)), (links.send(left, a=1), lambda i, k: (k, 1, i)),
        (right, lambda i, k: (k + 2, i, 0)), (links.send(right, b=1), lambda i, k: (k + 2, i, 1)),
    ]
    pieces = []
    for value, where in parts:
        for core, v in ((0, value), (1, links.send(value, core=1))):
            places = []
            for i in range(2):
                for k in range(2):
                    z, a, b = where(i, k)
                    places.append(((i, k), z, core, a, b))
            pieces.append((v, places))
    return pieces


def assemble_kernel(coords_ref, *refs, places, rows):
    *ins, out_ref, sem = refs
    copies = []
    for value, where in zip(ins, places, strict=True):
        for index, z, core, a, b in where:
            start = pl.multiple_of(owner(coords_ref, z, core, a, b) * rows, 8)
            copies.append(
                pltpu.make_async_copy(
                    value.at[index], out_ref.at[pl.ds(start, rows)], sem.at[len(copies)]
                )
            )
            copies[-1].start()
    for copy in copies:
        copy.wait()


def assemble(links, pieces, name):
    rows, cols = pieces[0][0].shape[-2:]
    anywhere = pl.BlockSpec(memory_space=pl.ANY)
    return pl.pallas_call(
        functools.partial(assemble_kernel, places=[p[1] for p in pieces], rows=rows),
        name=name,
        in_specs=[pl.BlockSpec(memory_space=pltpu.SMEM)] + [anywhere] * len(pieces),
        out_specs=pl.BlockSpec(memory_space=pltpu.VMEM),
        out_shape=jax.ShapeDtypeStruct((32 * rows, cols), BF16),
        scratch_shapes=[pltpu.SemaphoreType.DMA((32,))],
        compiler_params=params(),
        cost_estimate=pl.CostEstimate(
            flops=0, bytes_accessed=32 * rows * cols * 4, transcendentals=0
        ),
    )(links.coords, *[p[0] for p in pieces])


def send_order():
    order = []
    for core in range(2):
        order += [(core, a, b, k) for b in range(2) for a in range(2) for k in (0, 1)]
        order += [(core, a, b, k) for a in range(2) for b in range(2) for k in (2, 3)]
    return order


def deal_kernel(coords_ref, *refs, rows, spans):
    ins, keep_ref, away_ref, sem = refs[:-3], refs[-3], refs[-2], refs[-1]
    copies = []
    for at, (core, a, b, z) in enumerate(send_order()):
        dev = owner(coords_ref, 4 - z, core, a, b)
        start = pl.multiple_of(dev * rows, 8)
        out = away_ref if core else keep_ref
        for value, (lo, hi) in zip(ins, spans, strict=True):
            copies.append(
                pltpu.make_async_copy(
                    value.at[pl.ds(start, rows)],
                    out.at[at % 16, :, lo:hi],
                    sem.at[len(copies)],
                )
            )
            copies[-1].start()
    for copy in copies:
        copy.wait()


def deal(links, grads, rows, name):
    spans, at = [], 0
    for g in grads:
        spans.append((at, at + g.shape[1]))
        at += g.shape[1]
    anywhere = pl.BlockSpec(memory_space=pl.ANY)
    vmem = pl.BlockSpec(memory_space=pltpu.VMEM)
    return pl.pallas_call(
        functools.partial(deal_kernel, rows=rows, spans=spans),
        name=name,
        in_specs=[pl.BlockSpec(memory_space=pltpu.SMEM)] + [anywhere] * len(grads),
        out_specs=[vmem, vmem],
        out_shape=[jax.ShapeDtypeStruct((16, rows, at), BF16)] * 2,
        scratch_shapes=[pltpu.SemaphoreType.DMA((32 * len(grads),))],
        compiler_params=params(),
        cost_estimate=pl.CostEstimate(
            flops=0, bytes_accessed=32 * rows * at * 4, transcendentals=0
        ),
    )(links.coords, *grads)


def add(a, b):
    return (a.astype(F32) + b.astype(F32)).astype(BF16)


def reduce_blocks(links, keep, away):
    got = links.send(away, core=1)
    part = lambda lo, hi: add(keep[lo:hi], got[lo:hi])
    left_got = links.send(part(4, 8), b=1)
    right_got = links.send(part(12, 16), a=1)
    left, right = part(0, 4), part(8, 12)
    left_got2 = links.send(add(left[2:], left_got[2:]), a=1)
    right_got2 = links.send(add(right[2:], right_got[2:]), b=1)
    left, right = add(left[:2], left_got[:2]), add(right[:2], right_got[:2])
    one = links.send(add(left[1], left_got2[1]), z=1)
    two = links.send(add(right[0], right_got2[0]), z=2)
    three = links.send(add(right[1], right_got2[1]), z=3)
    total = left[0].astype(F32) + left_got2[0].astype(F32)
    return total + one.astype(F32) + two.astype(F32) + three.astype(F32)


def gather(value):
    return lax.all_gather(value, AXES, axis=0, tiled=True)


def scatter(value):
    return lax.psum_scatter(value, AXES, scatter_dimension=0, tiled=True)


SLOTS = 24


def vector_slots(vectors):
    rows = [jnp.pad(v, (0, LANES - v.shape[0])) for v in vectors]
    rows += [jnp.zeros((LANES,), vectors[0].dtype)] * (SLOTS - len(rows))
    return jnp.stack(rows)


def unslot(slots, sizes):
    return [slots[:, k, :m].reshape(1, -1) for k, m in enumerate(sizes)]


def on_device(
    embedded, first_drop, second_drop, sent_lengths, out_cotangent,
    triple_weight, query_value_bias, mixer_weight, mixer_bias, first_gain, first_shift,
    widen_weight, widen_bias, narrow_weight, narrow_bias, second_gain, second_shift,
    pooler_weight, pooler_bias,
):
    views, sents, length, d = embedded.shape
    n = views * sents * length
    seqs = views * sents
    ff = widen_weight.shape[1]
    devices = lax.axis_size(AXES)
    links = Links()
    near = links.square() and triple_weight.shape[0] == SLOTS
    x = embedded.reshape(n, d)
    drop1 = first_drop.reshape(n, d)
    drop2 = second_drop.reshape(n, d)
    cot = out_cotangent.reshape(n, d)

    small = [
        query_value_bias, mixer_bias, first_gain, first_shift, widen_bias, narrow_bias,
        second_gain, second_shift, pooler_bias,
    ]
    sizes = [v.shape[0] for v in small]
    slots = vector_slots(small)
    narrow_rows = narrow_weight.shape[0]
    if near:
        attn_block = jnp.concatenate([triple_weight, slots], axis=1)
        ffn_block = jnp.concatenate([widen_weight, mixer_weight, pooler_weight], axis=1)
        attn_pieces = spread_small(links, attn_block)
        attn_all = assemble(links, attn_pieces, "gather_attn")
        slots_all = attn_all[:, 3 * d :].reshape(devices, SLOTS, LANES)
        ffn_all = assemble(links, spread_large(links, spread_first(links, ffn_block)), "gather_ffn")
        wn = assemble(links, spread_large(links, spread_first(links, narrow_weight)), "gather_narrow")
    else:
        attn_all = gather(triple_weight)
        slots_all = gather(slots[None])
        ffn_all = gather(jnp.concatenate([widen_weight, mixer_weight, pooler_weight], axis=1))
        wn = gather(narrow_weight)
    qv, mb, g1, s1, wwb, wnb, g2, s2, wpb = unslot(slots_all.astype(F32), sizes)
    wb = jnp.concatenate([qv[:, :d], jnp.zeros((1, d), F32), qv[:, d:]], axis=1)

    packed, p, ctx, c1, rho1, c_first, sums1 = attn_fwd(
        sent_lengths, x, drop1, attn_all, wb, ffn_all, mb, length
    )
    drop_first = second_drop[:, :, 0].reshape(seqs, d)
    unit, pooled, rho_p, first = first_tokens(
        c_first, drop_first, g1, s1, ffn_all, wwb, wn, wnb, g2, s2, wpb
    )
    if near:
        units = assemble(links, spread_small(links, unit), "gather_units").reshape(devices, seqs, d)
    else:
        units = gather(unit[None])
    one = units[:, :sents].reshape(devices * sents, d)
    two = units[:, sents:].reshape(devices * sents, d)
    hl, act, slope, c2, rho2, outputs, sums2 = ffn_fwd(
        sent_lengths, c1, drop2, g1, s1, ffn_all, wwb, wn, wnb, g2, s2, length
    )
    loss, dfirst, g_pool, g_poolb = loss_parts(links.place, one, two, pooled, rho_p, first, ffn_all)
    dnarrow, dwide, dres, dbranch, rows, wide = ffn_back(
        sent_lengths, cot, dfirst, c2, rho2, drop2, slope, c1, rho1, drop1, g1, ffn_all, wn, g2, length
    )
    g_narrow = dot_tn(act, dnarrow).astype(BF16)
    g_widen = dot_tn(hl, dwide).astype(BF16)
    g_pool = g_pool.astype(BF16)
    if near:
        s_wn = reduce_blocks(links, *deal(links, [g_narrow], narrow_rows, "deal_narrow"))
        wide_sum = reduce_blocks(links, *deal(links, [g_widen, g_pool], SLOTS, "deal_widen"))
        s_ww, s_wp = wide_sum[:, :ff], wide_sum[:, ff:]
    g_mixer = dot_tn(ctx, dbranch).astype(BF16)
    dpacked, dx, packed_sums = attn_back(dbranch, dres, packed, p, attn_all, ffn_all)
    g_triple = dot_tn(x, dpacked).astype(BF16)

    count = 2.0 * jnp.sum(sent_lengths).astype(F32)
    sq = [jnp.sum(sums1[:, 0]), jnp.sum(sums1[:, 1]), jnp.sum(sums2), count]
    qvg = jnp.concatenate([packed_sums[0, :d], packed_sums[0, 2 * d :]])
    vec = [qvg, rows[5], rows[3], rows[4], wide[0], rows[2], rows[0], rows[1], g_poolb[0]]
    vec = [jnp.pad(v.reshape(devices, -1), ((0, 0), (0, LANES - m))) for v, m in zip(vec, sizes)]
    vec += [jnp.broadcast_to(v, (devices, LANES)) for v in sq]
    vec += [jnp.zeros((devices, LANES), F32)] * (SLOTS - len(vec))
    vec = jnp.stack(vec, axis=1)
    if near:
        vec = vec.reshape(devices * SLOTS, LANES).astype(BF16)
        attn_sum = reduce_blocks(links, *deal(links, [g_triple, g_mixer, vec], SLOTS, "deal_attn"))
        s_w, s_m, got = attn_sum[:, : 3 * d], attn_sum[:, 3 * d : 4 * d], attn_sum[:, 4 * d :]
    else:
        s_w, s_m, s_ww, s_wn, s_wp = (
            scatter(g).astype(F32) for g in (g_triple, g_mixer, g_widen, g_narrow, g_pool)
        )
        got = scatter(vec)[0]
    sums = got[len(small) : len(small) + 4, 0]
    rms = jnp.sqrt(sums[:3] / (sums[3] * d))
    got = [got[k, :m] for k, m in enumerate(sizes)]
    return (
        loss[0, 0], outputs.reshape(embedded.shape), dx.reshape(embedded.shape), rms,
        s_w, got[0], s_m, got[1], got[2], got[3], s_ww, got[4], s_wn, got[5], got[6], got[7],
        s_wp, got[8],
    )


def solution(mesh):
    rows4 = P(None, AXES, None, None)
    mat, vec = P(AXES, None), P(AXES)
    in_specs = (
        rows4, rows4, rows4, vec, rows4,
        mat, vec, mat, vec, vec, vec, mat, vec, mat, vec, vec, vec, mat, vec,
    )
    out_specs = (
        P(), rows4, rows4, P(), mat, vec, mat, vec, vec, vec, mat, vec, mat, vec, vec, vec, mat, vec,
    )
    return jax.shard_map(
        on_device, mesh=mesh, in_specs=in_specs, out_specs=out_specs, check_vma=False
    )
```

time: 1170 us -> 572 us (0.49)
  waiting for transfers between devices: 482 us -> 167 us
  matrix products: 310 us -> 49.8 us
  Pallas kernels: 0 us -> 216 us
  local copies, waits for them, and re-layouts: 156 us -> 33.5 us
  other arithmetic: 111 us -> 17.3 us
  blocking collectives: 83.6 us -> 0 us
  starting transfers between devices: 0.48 us -> 75.6 us
  between operations: 18.3 us -> 3.35 us
    reduce_scatter x5 -> x0, waiting for transfers between devices: 378 us -> none  [the longest x1 142 us: on_device(): lax.psum_scatter(grad_narrow_weight, ('fsdp', 'dp'), scatter_dimension=0,...]
    dot_general x24 -> x4, matrix products: 310 us -> 49.8 us  [dot_tn(): lax.dot_general(a, b, (((0,), (0,)), ((), ())), preferred_element_type=F32)]
    pallas_call x0 -> x13, Pallas kernels: none -> 216 us  [the longest x1 51.2 us: attn_back(): pl.pallas_call(attn_back_kernel, name='attn_back', grid=(n // ROWS,), in_...]
    ppermute x0 -> x66, waiting for transfers between devices: none -> 167 us  [send(): return lax.ppermute(value, AXES, pairs)]
    ppermute x0 -> x66, starting transfers between devices: none -> 75.6 us  [send(): return lax.ppermute(value, AXES, pairs)]
    convert_element_type x4 -> x0, local copies, waits for them, and re-layouts: 66.4 us -> none  [the longest x2 43.5 us: on_device(): dpacked = jnp.stack([dqueries, dkey_rows, dvalues], axis=2).astype(jnp.bf...]
    all_gather x6 -> x0, waiting for transfers between devices: 61.9 us -> none  [the longest x1 54.8 us: on_device(): lax.all_gather(second_unit, ('fsdp', 'dp'), axis=0, tiled=True)]
    reduce_sum x14 -> x3, other arithmetic: 55.9 us -> 2.61 us  [the longest x2 1.98 us: on_device(): sq = [jnp.sum(sums1[:, 0]), jnp.sum(sums1[:, 1]), jnp.sum(sums2), count]]
  transfers between devices with their start and end apart: 12 -> 66, of which waited for: 6 -> 26; matrix products, arithmetic and copies ran while one was open for 48% -> 12% of each run, Pallas kernels for 0% -> 11%
where the time goes in v1:
time: 572 us; the launch traced here: 563 us
  Pallas kernels  216 us (38%)
  waiting for transfers between devices  167 us (29%)
  starting transfers between devices  75.6 us (13%)
  matrix products  49.8 us (9%)
  local copies, waits for them, and re-layouts  33.5 us (6%)
  other arithmetic  17.3 us (3%)
    ppermute x66, waiting for transfers between devices, send(): return lax.ppermute(value, AXES, pairs)  167 us
    ppermute x66, starting transfers between devices, send(): return lax.ppermute(value, AXES, pairs)  75.6 us
    pallas_call x1, Pallas kernels, attn_back(): pl.pallas_call(attn_back_kernel, name='attn_back', grid=(n // ROWS,), in_...  51.2 us
    dot_general x4, matrix products, dot_tn(): lax.dot_general(a, b, (((0,), (0,)), ((), ())), preferred_element_type=F32)  49.8 us
    pallas_call x1, Pallas kernels, ffn_back(): pl.pallas_call(functools.partial(ffn_back_kernel, length=length), name='f...  41 us
    pallas_call x1, Pallas kernels, ffn_fwd(): pl.pallas_call(functools.partial(ffn_fwd_kernel, length=length), name='ff...  38.6 us
    pallas_call x1, Pallas kernels, attn_fwd(): pl.pallas_call(functools.partial(attn_fwd_kernel, length=length), name='a...  28.9 us
    pallas_call x4, Pallas kernels, assemble(): pl.pallas_call(functools.partial(assemble_kernel, places=[p[1] for p in p...  22.2 us
  transfers between devices with their start and end apart: 66, of which 26 were waited for; matrix products, arithmetic and copies ran while one was open for 12% of the time, Pallas kernels for 11%

profile of v1, /device:TPU:0, one launch (start us, length us, event | category | flops | bytes accessed | tf_op | source)
XLA Modules:
  0.0 563.3 jit_solution(6486498072891475779)
XLA Ops:
  23.0 11.9 %collective-permute-start.15 = (bf16[24,4608]{1,0:T(8,128)(2,1)S(1)}, bf16[24,4608]{1,0:T(8,128)(2,1)S(1)}, u32[]{:S(2)}, u32[]{:S(2)}) collective-permute-start(bf16[24,4608]{1,0:T(8,128)(2,1)S(1)} %constant_dynamic-update-slice_fusion), channel_id=1, source_target_pairs={{0,16},{1,17},{2,18},{3,19},{4,20},{5,21},{6,22},{7,23},{8,24},{9,... | collective-permute-start | bytes 663560 | tf_op jit(solution)/shard_map/ppermute | solution.py:512
  40.3 8.1 %collective-permute-done.15 = bf16[24,4608]{1,0:T(8,128)(2,1)S(1)} collective-permute-done((bf16[24,4608]{1,0:T(8,128)(2,1)S(1)}, bf16[24,4608]{1,0:T(8,128)(2,1)S(1)}, u32[]{:S(2)}, u32[]{:S(2)}) %collective-permute-start.15) | collective-permute-done | bytes 221216 | tf_op jit(solution)/shard_map/ppermute | solution.py:512
  51.6 12.4 %collective-permute-done.28 = bf16[2,96,768]{2,1,0:T(8,128)(2,1)S(1)} collective-permute-done((bf16[2,96,768]{2,1,0:T(8,128)(2,1)S(1)}, bf16[2,96,768]{2,1,0:T(8,128)(2,1)S(1)}, u32[]{:S(2)}, u32[]{:S(2)}) %collective-permute-start.28) | collective-permute-done | bytes 294944 | tf_op jit(solution)/shard_map/ppermute | solution.py:512
  66.3 7.1 %collective-permute-done.17 = bf16[2,24,4608]{2,1,0:T(8,128)(2,1)S(1)} collective-permute-done((bf16[2,24,4608]{2,1,0:T(8,128)(2,1)S(1)}, bf16[2,24,4608]{2,1,0:T(8,128)(2,1)S(1)}, u32[]{:S(2)}, u32[]{:S(2)}) %collective-permute-start.17) | collective-permute-done | bytes 442400 | tf_op jit(solution)/shard_map/ppermute | solution.py:512
  77.7 9.4 %collective-permute-done.11 = bf16[2,24,4608]{2,1,0:T(8,128)(2,1)S(1)} collective-permute-done((bf16[2,24,4608]{2,1,0:T(8,128)(2,1)S(1)}, bf16[2,24,4608]{2,1,0:T(8,128)(2,1)S(1)}, u32[]{:S(2)}, u32[]{:S(2)}) %collective-permute-start.11) | collective-permute-done | bytes 442400 | tf_op jit(solution)/shard_map/ppermute | solution.py:512
  87.9 11.7 %collective-permute-done.30.refs_6_ = bf16[2,2,96,768]{3,2,1,0:T(8,128)(2,1)S(1)} collective-permute-done((bf16[2,2,96,768]{3,2,1,0:T(8,128)(2,1)S(1)}, bf16[2,2,96,768]{3,2,1,0:T(8,128)(2,1)S(1)}, u32[]{:S(2)}, u32[]{:S(2)}) %collective-permute-start.30) | collective-permute-done | bytes 589856 | tf_op jit(solution)/shard_map/ppermute | solution.py:512
  109.4 6.6 %collective-permute-done.19.refs_6_ = bf16[2,2,24,4608]{3,2,1,0:T(8,128)(2,1)} collective-permute-done((bf16[2,2,24,4608]{3,2,1,0:T(8,128)(2,1)S(1)}, bf16[2,2,24,4608]{3,2,1,0:T(8,128)(2,1)}, u32[]{:S(2)}, u32[]{:S(2)}) %collective-permute-start.19) | collective-permute-done | bytes 884768 | tf_op jit(solution)/shard_map/ppermute | solution.py:512
  130.3 5.5 gather_narrow.1.wn_ref
  135.9 7.0 %gather_ffn.1.m_ref.ww_ref.wp_ref = bf16[768,4608]{1,0:T(8,128)(2,1)} custom-call(s32[4]{0:T(128)} %pad_add_fusion.coords_ref, bf16[2,2,24,4608]{3,2,1,0:T(8,128)(2,1)} %copy-done.1, bf16[2,2,24,4608]{3,2,1,0:T(8,128)(2,1)} %collective-permute-done.12.refs_1_, bf16[2,2,24,4608]{3,2,1,0:T(8,128)(2,1)} %collective-permute-done.13.refs_2_, ...), custom_call_target="tpu_custom_call" | custom-call | bytes 14155776 | tf_op jit(solution)/shard_map/gather_ffn/pallas_call | solution.py:576
  142.9 28.9 %attn_fwd.1 = (bf16[2048,2304]{1,0:T(8,128)(2,1)}, bf16[2048,1536]{1,0:T(8,128)(2,1)}, bf16[2048,768]{1,0:T(8,128)(2,1)}, f32[2048,768]{1,0:T(8,128)}, f32[2048,...) custom-call(s32[32]{0:T(128)} %lens_ref.5, bf16[2048,768]{1,0:T(8,128)(2,1)} %bitcast.217, ...), custom_call_target="tpu_custom_call" | custom-call | flops 14495514624 | bytes 40894464 | tf_op jit(solution)/shard_map/attn_fwd/pallas_call | solution.py:161
  171.8 7.8 %first_tokens.1 = (bf16[64,768]{1,0:T(8,128)(2,1)}, f32[64,768]{1,0:T(8,128)}, f32[64,1]{1,0:T(8,128)}, bf16[64,768]{1,0:T(8,128)(2,1)}) custom-call(f32[64,768]{1,0:T(8,128)} %get-tuple-element.55.c_ref, s32[64,768]{1,0:T(8,128)} %bitcast.179, f32[1,768]{1,0:T(1,128)} %reshape_squeeze.65.g1_ref, f32[1,768]{1,0:T(1,128)} %reshape_squeeze.66.s1_ref, ...), custom_call_target="tpu_custom_call" | custom-call | tf_op jit(solution)/shard_map/first_tokens/pallas_call | solution.py:284
  179.6 7.7 %collective-permute-start.34 = (bf16[64,768]{1,0:T(8,128)(2,1)}, bf16[64,768]{1,0:T(8,128)(2,1)S(1)}, u32[]{:S(2)}, u32[]{:S(2)}) collective-permute-start(bf16[64,768]{1,0:T(8,128)(2,1)} %get-tuple-element.56), channel_id=1, source_target_pairs={{0,24},{1,25},{2,26},{3,27},{4,28},{5,29},{6,30},{7,31},{8,0},{9,1... | collective-permute-start | bytes 294920 | tf_op jit(solution)/shard_map/ppermute | solution.py:512
  190.8 5.8 %collective-permute-done.33 = bf16[64,768]{1,0:T(8,128)(2,1)S(1)} collective-permute-done((bf16[64,768]{1,0:T(8,128)(2,1)}, bf16[64,768]{1,0:T(8,128)(2,1)S(1)}, u32[]{:S(2)}, u32[]{:S(2)}) %collective-permute-start.33) | collective-permute-done | bytes 98336 | tf_op jit(solution)/shard_map/ppermute | solution.py:512
  202.5 8.1 %collective-permute-done.40.refs_6_ = bf16[4,64,768]{2,1,0:T(8,128)(2,1)S(1)} collective-permute-done((bf16[4,64,768]{2,1,0:T(8,128)(2,1)S(1)}, bf16[4,64,768]{2,1,0:T(8,128)(2,1)S(1)}, u32[]{:S(2)}, u32[]{:S(2)}) %collective-permute-start.40) | collective-permute-done | bytes 393248 | tf_op jit(solution)/shard_map/ppermute | solution.py:512
  210.5 7.2 %collective-permute-done.38.refs_4_ = bf16[4,64,768]{2,1,0:T(8,128)(2,1)S(1)} collective-permute-done((bf16[4,64,768]{2,1,0:T(8,128)(2,1)S(1)}, bf16[4,64,768]{2,1,0:T(8,128)(2,1)S(1)}, u32[]{:S(2)}, u32[]{:S(2)}) %collective-permute-start.38) | collective-permute-done | bytes 393248 | tf_op jit(solution)/shard_map/ppermute | solution.py:512
  218.3 38.6 %ffn_fwd.1 = (bf16[2048,768]{1,0:T(8,128)(2,1)}, bf16[2048,3072]{1,0:T(8,128)(2,1)}, bf16[2048,3072]{1,0:T(8,128)(2,1)}, f32[2048,768]{1,0:T(8,128)}, f32[2048,1...) custom-call(s32[32]{0:T(128)} %lens_ref.5, f32[2048,768]{1,0:T(8,128)} %get-tuple-element.61.c_ref, ...), custom_call_target="tpu_custom_call" | custom-call | flops 19327352832 | bytes 50331648 | tf_op jit(solution)/shard_map/ffn_fwd/pallas_call | solution.py:229
  269.3 8.0 %loss.1 = (f32[1,1]{1,0:T(1,128)}, f32[64,768]{1,0:T(8,128)}, f32[768,768]{1,0:T(8,128)}, f32[1,768]{1,0:T(1,128)}) custom-call(s32[1]{0:T(128)} %bitcast.place_ref, bf16[1024,768]{1,0:T(8,128)(2,1)} %bitcast.178, bf16[1024,768]{1,0:T(8,128)(2,1)} %bitcast.177, f32[64,768]{1,0:T(8,128)} %get-tuple-element.57.pooled_ref, f32[64,1]{1,0:T(8,128)} %get-tuple-element.58.rho_ref, ...), custom_call_target="tpu_custom_call" | custom-call | tf_op jit(solution)/shard_map/loss/pallas_call | solution.py:339
  278.2 41.0 %ffn_back.1 = (bf16[2048,768]{1,0:T(8,128)(2,1)}, bf16[2048,3072]{1,0:T(8,128)(2,1)}, f32[2048,768]{1,0:T(8,128)}, bf16[2048,768]{1,0:T(8,128)(2,1)}, f32[8,768]{1,0:T(8,128)}, /*index=5*/f32[8,3072]{1,0:T(8,128)}) custom-call(s32[32]{0:T(128)} %lens_ref.5, bf16[2048,768]{1,0:T(8,128)(2,1)} %bitcast.216, f32[64,768]{1,0:T(8,128)} %get-tuple-element.63.dfirst_ref, ...), custom_call_target="tpu_custom_call" | custom-call | flops 19327352832 | bytes 62914560 | tf_op jit(solution)/shard_map/ffn_back/pallas_call | solution.py:406
  319.2 15.7 %convolution_convert_fusion.refs_0_ = bf16[3072,768]{1,0:T(8,128)(2,1)} fusion(bf16[2048,3072]{1,0:T(8,128)(2,1)} %get-tuple-element.88, bf16[2048,768]{1,0:T(8,128)(2,1)} %get-tuple-element.89), kind=kOutput, calls=%fused_computation | convolution fusion | flops 9666035712 | bytes 20447232 | tf_op jit(solution)/shard_map/dot_general | solution.py:35
  334.9 5.9 %deal_narrow.1 = (bf16[16,96,768]{2,1,0:T(8,128)(2,1)}, bf16[16,96,768]{2,1,0:T(8,128)(2,1)}) custom-call(s32[4]{0:T(128)} %pad_add_fusion.coords_ref, bf16[3072,768]{1,0:T(8,128)(2,1)} %convolution_convert_fusion.refs_0_), custom_call_target="tpu_custom_call" | custom-call | bytes 9437184 | tf_op jit(solution)/shard_map/deal_narrow/pallas_call | solution.py:625
  342.7 5.6 convolution_convert_fusion.3.refs_1_
  348.3 51.2 %attn_back.1 = (bf16[2048,2304]{1,0:T(8,128)(2,1)}, bf16[2048,768]{1,0:T(8,128)(2,1)}, f32[8,2304]{1,0:T(8,128)}) custom-call(bf16[2048,768]{1,0:T(8,128)(2,1)} %get-tuple-element.68.dbranch_ref, f32[2048,768]{1,0:T(8,128)} %get-tuple-element.69.dres_ref, bf16[2048,2304]{1,0:T(8,128)(2,1)} %get-tuple-element.70.packed_ref, ...), custom_call_target="tpu_custom_call" | custom-call | flops 19327352832 | bytes 37748736 | tf_op jit(solution)/shard_map/attn_back/pallas_call | solution.py:477
  401.0 12.8 %fusion.refs_0_ = bf16[768,2304]{1,0:T(8,128)(2,1)} fusion(bf16[2048,2304]{1,0:T(8,128)(2,1)} %get-tuple-element.73, bf16[2048,768]{1,0:T(8,128)(2,1)S(1)} %bitcast.218), kind=kOutput, calls=%fused_computation.3 | convolution fusion | flops 7249526784 | bytes 16121856 | tf_op jit(solution)/shard_map/dot_general | solution.py:35
  418.1 6.3 %deal_attn.1 = (bf16[16,24,3200]{2,1,0:T(8,128)(2,1)}, bf16[16,24,3200]{2,1,0:T(8,128)(2,1)}) custom-call(s32[4]{0:T(128)} %pad_add_fusion.coords_ref, bf16[768,2304]{1,0:T(8,128)(2,1)} %fusion.refs_0_, bf16[768,768]{1,0:T(8,128)(2,1)} %convolution_convert_fusion.3.refs_1_, bf16[768,128]{1,0:T(8,128)(2,1)} %bitcast.180), custom_call_target="tpu_custom_call" | custom-call | bytes 9830400 | tf_op jit(solution)/shard_map/deal_attn/pallas_call | solution.py:625
  424.7 15.8 %convolution_convert_fusion.1.refs_0_ = bf16[768,3072]{1,0:T(8,128)(2,1)} fusion(bf16[2048,768]{1,0:T(8,128)(2,1)} %get-tuple-element.83, bf16[2048,3072]{1,0:T(8,128)(2,1)} %get-tuple-element.84), kind=kOutput, calls=%fused_computation.1 | convolution fusion | flops 9666035712 | bytes 20447232 | tf_op jit(solution)/shard_map/dot_general | solution.py:35
  441.6 6.6 %deal_widen.1 = (bf16[16,24,3840]{2,1,0:T(8,128)(2,1)}, bf16[16,24,3840]{2,1,0:T(8,128)(2,1)}) custom-call(s32[4]{0:T(128)} %pad_add_fusion.coords_ref, bf16[768,3072]{1,0:T(8,128)(2,1)} %convolution_convert_fusion.1.refs_0_, bf16[768,768]{1,0:T(8,128)(2,1)} %convert_element_type.495.refs_1_), custom_call_target="tpu_custom_call" | custom-call | bytes 11796480 | tf_op jit(solution)/shard_map/deal_widen/pallas_call | solution.py:625
  456.4 11.5 %collective-permute-done.62 = bf16[4,96,768]{2,1,0:T(8,128)(2,1)S(1)} collective-permute-done((bf16[4,96,768]{2,1,0:T(8,128)(2,1)S(1)}, bf16[4,96,768]{2,1,0:T(8,128)(2,1)S(1)}, u32[]{:S(2)}, u32[]{:S(2)}) %collective-permute-start.62) | collective-permute-done | bytes 589856 | tf_op jit(solution)/shard_map/ppermute | solution.py:512
  472.7 8.3 %collective-permute-done.46 = bf16[4,24,3200]{2,1,0:T(8,128)(2,1)S(1)} collective-permute-done((bf16[4,24,3200]{2,1,0:T(8,128)(2,1)S(1)}, bf16[4,24,3200]{2,1,0:T(8,128)(2,1)S(1)}, u32[]{:S(2)}, u32[]{:S(2)}) %collective-permute-start.46) | collective-permute-done | bytes 614432 | tf_op jit(solution)/shard_map/ppermute | solution.py:512
  491.0 19.5 %collective-permute-done.47 = bf16[2,24,3200]{2,1,0:T(8,128)(2,1)S(1)} collective-permute-done((bf16[2,24,3200]{2,1,0:T(8,128)(2,1)S(1)}, bf16[2,24,3200]{2,1,0:T(8,128)(2,1)S(1)}, u32[]{:S(2)}, u32[]{:S(2)}) %collective-permute-start.47) | collective-permute-done | bytes 307232 | tf_op jit(solution)/shard_map/ppermute | solution.py:512
  536.3 6.3 %collective-permute-done.55 = bf16[2,24,3840]{2,1,0:T(8,128)(2,1)S(1)} collective-permute-done((bf16[2,24,3840]{2,1,0:T(8,128)(2,1)S(1)}, bf16[2,24,3840]{2,1,0:T(8,128)(2,1)S(1)}, u32[]{:S(2)}, u32[]{:S(2)}) %collective-permute-start.55) | collective-permute-done | bytes 368672 | tf_op jit(solution)/shard_map/ppermute | solution.py:512
  542.7 5.6 collective-permute-start.56
  550.9 7.0 %collective-permute-done.56 = bf16[24,3840]{1,0:T(8,128)(2,1)S(1)} collective-permute-done((bf16[24,3840]{1,0:T(8,128)(2,1)S(1)}, bf16[24,3840]{1,0:T(8,128)(2,1)S(1)}, u32[]{:S(2)}, u32[]{:S(2)}) %collective-permute-start.56) | collective-permute-done | bytes 184352 | tf_op jit(solution)/shard_map/ppermute | solution.py:512
  (293 shorter events, 149.4 us)
Async XLA Ops:
  0.7 36.5 %collective-permute-start.21 = (bf16[96,768]{1,0:T(8,128)(2,1)}, bf16[96,768]{1,0:T(8,128)(2,1)S(1)}, u32[]{:S(2)}, u32[]{:S(2)}) collective-permute-start(bf16[96,768]{1,0:T(8,128)(2,1)} %param.32), channel_id=1, source_target_pairs={{0,8},{1,9},{2,10},{3,11},{4,12},{5,13},{6,14},{7,15},{8,16},{9,17... | collective-permute-start | bytes 442376 | tf_op jit(solution)/shard_map/ppermute | solution.py:512
  3.7 31.3 %collective-permute-start.27 = (bf16[96,768]{1,0:T(8,128)(2,1)}, bf16[96,768]{1,0:T(8,128)(2,1)S(1)}, u32[]{:S(2)}, u32[]{:S(2)}) collective-permute-start(bf16[96,768]{1,0:T(8,128)(2,1)} %param.32), channel_id=1, source_target_pairs={{0,24},{1,25},{2,26},{3,27},{4,28},{5,29},{6,30},{7,31},{8,0},{9,1... | collective-permute-start | bytes 442376 | tf_op jit(solution)/shard_map/ppermute | solution.py:512
  23.0 25.3 %collective-permute-start.15 = (bf16[24,4608]{1,0:T(8,128)(2,1)S(1)}, bf16[24,4608]{1,0:T(8,128)(2,1)S(1)}, u32[]{:S(2)}, u32[]{:S(2)}) collective-permute-start(bf16[24,4608]{1,0:T(8,128)(2,1)S(1)} %constant_dynamic-update-slice_fusion), channel_id=1, source_target_pairs={{0,16},{1,17},{2,18},{3,19},{4,20},{5,21},{6,22},{7,23},{8,24},{9,... | collective-permute-start | bytes 663560 | tf_op jit(solution)/shard_map/ppermute | solution.py:512
  37.1 27.1 %collective-permute-start.8 = (bf16[4,24,2432]{2,1,0:T(8,128)(2,1)S(1)}, bf16[4,24,2432]{2,1,0:T(8,128)(2,1)S(1)}, u32[]{:S(2)}, u32[]{:S(2)}) collective-permute-start(bf16[4,24,2432]{2,1,0:T(8,128)(2,1)S(1)} %pad_maximum_fusion.4.refs_0_), channel_id=1, source_target_pairs={{0,3},{1,2},{2,1},{3,0},{4,7},{5,6},{6,5},{7,4},{8,11},{9,10},{10,... | collective-permute-start | bytes 1400840 | tf_op jit(solution)/shard_map/ppermute | solution.py:512
  37.2 29.1 %collective-permute-start.6 = (bf16[4,24,2432]{2,1,0:T(8,128)(2,1)S(1)}, bf16[4,24,2432]{2,1,0:T(8,128)(2,1)}, u32[]{:S(2)}, u32[]{:S(2)}) collective-permute-start(bf16[4,24,2432]{2,1,0:T(8,128)(2,1)S(1)} %pad_maximum_fusion.4.refs_0_), channel_id=1, source_target_pairs={{0,2},{1,3},{2,0},{3,1},{4,6},{5,7},{6,4},{7,5},{8,10},{9,11},{10,... | collective-permute-start | bytes 1400840 | tf_op jit(solution)/shard_map/ppermute | solution.py:512
  38.2 25.7 %collective-permute-start.28 = (bf16[2,96,768]{2,1,0:T(8,128)(2,1)S(1)}, bf16[2,96,768]{2,1,0:T(8,128)(2,1)S(1)}, u32[]{:S(2)}, u32[]{:S(2)}) collective-permute-start(bf16[2,96,768]{2,1,0:T(8,128)(2,1)S(1)} %get-tuple-element.146), channel_id=1, source_target_pairs={{0,2},{1,3},{2,0},{3,1},{4,6},{5,7},{6,4},{7,5},{8,10},{9,11},{10,... | collective-permute-start | bytes 884744 | tf_op jit(solution)/shard_map/ppermute | solution.py:512
  49.9 23.5 %collective-permute-start.17 = (bf16[2,24,4608]{2,1,0:T(8,128)(2,1)S(1)}, bf16[2,24,4608]{2,1,0:T(8,128)(2,1)S(1)}, u32[]{:S(2)}, u32[]{:S(2)}) collective-permute-start(bf16[2,24,4608]{2,1,0:T(8,128)(2,1)S(1)} %get-tuple-element.135), channel_id=1, source_target_pairs={{0,2},{1,3},{2,0},{3,1},{4,6},{5,7},{6,4},{7,5},{8,10},{9,11},{10,... | collective-permute-start | bytes 1327112 | tf_op jit(solution)/shard_map/ppermute | solution.py:512
  64.2 22.8 %collective-permute-start.11 = (bf16[2,24,4608]{2,1,0:T(8,128)(2,1)S(1)}, bf16[2,24,4608]{2,1,0:T(8,128)(2,1)S(1)}, u32[]{:S(2)}, u32[]{:S(2)}) collective-permute-start(bf16[2,24,4608]{2,1,0:T(8,128)(2,1)S(1)} %get-tuple-element.137), channel_id=1, source_target_pairs={{0,1},{1,0},{2,3},{3,2},{4,5},{5,4},{6,7},{7,6},{8,9},{9,8},{10,11... | collective-permute-start | bytes 1327112 | tf_op jit(solution)/shard_map/ppermute | solution.py:512
  66.3 20.9 %collective-permute-start.24 = (bf16[2,2,96,768]{3,2,1,0:T(8,128)(2,1)S(1)}, bf16[2,2,96,768]{3,2,1,0:T(8,128)(2,1)}, u32[]{:S(2)}, u32[]{:S(2)}) collective-permute-start(bf16[2,2,96,768]{3,2,1,0:T(8,128)(2,1)S(1)} %pad_maximum_fusion.2.refs_0_), channel_id=1, source_target_pairs={{0,2},{1,3},{2,0},{3,1},{4,6},{5,7},{6,4},{7,5},{8,10},{9,11},{10,... | collective-permute-start | bytes 1769480 | tf_op jit(solution)/shard_map/ppermute | solution.py:512
  77.7 22.0 %collective-permute-start.30 = (bf16[2,2,96,768]{3,2,1,0:T(8,128)(2,1)S(1)}, bf16[2,2,96,768]{3,2,1,0:T(8,128)(2,1)S(1)}, u32[]{:S(2)}, u32[]{:S(2)}) collective-permute-start(bf16[2,2,96,768]{3,2,1,0:T(8,128)(2,1)S(1)} %pad_maximum_fusion.3.refs_4_), channel_id=1, source_target_pairs={{0,1},{1,0},{2,3},{3,2},{4,5},{5,4},{6,7},{7,6},{8,9},{9,8},{10,11... | collective-permute-start | bytes 1769480 | tf_op jit(solution)/shard_map/ppermute | solution.py:512
  77.7 22.0 %collective-permute-start.29 = (bf16[2,2,96,768]{3,2,1,0:T(8,128)(2,1)S(1)}, bf16[2,2,96,768]{3,2,1,0:T(8,128)(2,1)S(1)}, u32[]{:S(2)}, u32[]{:S(2)}) collective-permute-start(bf16[2,2,96,768]{3,2,1,0:T(8,128)(2,1)S(1)} %pad_maximum_fusion.3.refs_4_), channel_id=1, source_target_pairs={{0,4},{1,5},{2,6},{3,7},{4,0},{5,1},{6,2},{7,3},{8,12},{9,13},{10,... | collective-permute-start | bytes 1769480 | tf_op jit(solution)/shard_map/ppermute | solution.py:512
  87.1 22.2 %collective-permute-start.13 = (bf16[2,2,24,4608]{3,2,1,0:T(8,128)(2,1)S(1)}, bf16[2,2,24,4608]{3,2,1,0:T(8,128)(2,1)}, u32[]{:S(2)}, u32[]{:S(2)}) collective-permute-start(bf16[2,2,24,4608]{3,2,1,0:T(8,128)(2,1)S(1)} %pad_maximum_fusion.refs_0_), channel_id=1, source_target_pairs={{0,2},{1,3},{2,0},{3,1},{4,6},{5,7},{6,4},{7,5},{8,10},{9,11},{10,... | collective-permute-start | bytes 2654216 | tf_op jit(solution)/shard_map/ppermute | solution.py:512
  87.2 28.7 %collective-permute-start.19 = (bf16[2,2,24,4608]{3,2,1,0:T(8,128)(2,1)S(1)}, bf16[2,2,24,4608]{3,2,1,0:T(8,128)(2,1)}, u32[]{:S(2)}, u32[]{:S(2)}) collective-permute-start(bf16[2,2,24,4608]{3,2,1,0:T(8,128)(2,1)S(1)} %pad_maximum_fusion.1.refs_4_), channel_id=1, source_target_pairs={{0,1},{1,0},{2,3},{3,2},{4,5},{5,4},{6,7},{7,6},{8,9},{9,8},{10,11... | collective-permute-start | bytes 2654216 | tf_op jit(solution)/shard_map/ppermute | solution.py:512
  99.7 23.0 %collective-permute-start.25 = (bf16[2,2,96,768]{3,2,1,0:T(8,128)(2,1)}, bf16[2,2,96,768]{3,2,1,0:T(8,128)(2,1)}, u32[]{:S(2)}, u32[]{:S(2)}) collective-permute-start(bf16[2,2,96,768]{3,2,1,0:T(8,128)(2,1)} %collective-permute-done.24.refs_2_), channel_id=1, source_target_pairs={{0,4},{1,5},{2,6},{3,7},{4,0},{5,1},{6,2},{7,3},{8,12},{9,13},{10,... | collective-permute-start | bytes 1769480 | tf_op jit(solution)/shard_map/ppermute | solution.py:512
  103.7 32.1 %collective-permute-start.12 = (bf16[2,2,24,4608]{3,2,1,0:T(8,128)(2,1)S(1)}, bf16[2,2,24,4608]{3,2,1,0:T(8,128)(2,1)}, u32[]{:S(2)}, u32[]{:S(2)}) collective-permute-start(bf16[2,2,24,4608]{3,2,1,0:T(8,128)(2,1)S(1)} %pad_maximum_fusion.refs_0_), channel_id=1, source_target_pairs={{0,4},{1,5},{2,6},{3,7},{4,0},{5,1},{6,2},{7,3},{8,12},{9,13},{10,... | collective-permute-start | bytes 2654216 | tf_op jit(solution)/shard_map/ppermute | solution.py:512
  104.1 31.7 %collective-permute-start.18 = (bf16[2,2,24,4608]{3,2,1,0:T(8,128)(2,1)S(1)}, bf16[2,2,24,4608]{3,2,1,0:T(8,128)(2,1)}, u32[]{:S(2)}, u32[]{:S(2)}) collective-permute-start(bf16[2,2,24,4608]{3,2,1,0:T(8,128)(2,1)S(1)} %pad_maximum_fusion.1.refs_4_), channel_id=1, source_target_pairs={{0,4},{1,5},{2,6},{3,7},{4,0},{5,1},{6,2},{7,3},{8,12},{9,13},{10,... | collective-permute-start | bytes 2654216 | tf_op jit(solution)/shard_map/ppermute | solution.py:512
  109.4 26.5 %collective-permute-start.14 = (bf16[2,2,24,4608]{3,2,1,0:T(8,128)(2,1)}, bf16[2,2,24,4608]{3,2,1,0:T(8,128)(2,1)}, u32[]{:S(2)}, u32[]{:S(2)}) collective-permute-start(bf16[2,2,24,4608]{3,2,1,0:T(8,128)(2,1)} %collective-permute-done.13.refs_2_), channel_id=1, source_target_pairs={{0,4},{1,5},{2,6},{3,7},{4,0},{5,1},{6,2},{7,3},{8,12},{9,13},{10,... | collective-permute-start | bytes 2654216 | tf_op jit(solution)/shard_map/ppermute | solution.py:512
  202.4 56.5 %collective-permute-start.35 = (bf16[4,64,768]{2,1,0:T(8,128)(2,1)S(1)}, bf16[4,64,768]{2,1,0:T(8,128)(2,1)S(1)}, u32[]{:S(2)}, u32[]{:S(2)}) collective-permute-start(bf16[4,64,768]{2,1,0:T(8,128)(2,1)S(1)} %pad_maximum_fusion.7.refs_0_), channel_id=1, source_target_pairs={{0,4},{1,5},{2,6},{3,7},{4,0},{5,1},{6,2},{7,3},{8,12},{9,13},{10,... | collective-permute-start | bytes 1179656 | tf_op jit(solution)/shard_map/ppermute | solution.py:512
  210.5 48.3 %collective-permute-start.41 = (bf16[4,64,768]{2,1,0:T(8,128)(2,1)S(1)}, bf16[4,64,768]{2,1,0:T(8,128)(2,1)S(1)}, u32[]{:S(2)}, u32[]{:S(2)}) collective-permute-start(bf16[4,64,768]{2,1,0:T(8,128)(2,1)S(1)} %collective-permute-done.40.refs_6_), channel_id=1, source_target_pairs={{0,4},{1,5},{2,6},{3,7},{4,0},{5,1},{6,2},{7,3},{8,12},{9,13},{10,... | collective-permute-start | bytes 1179656 | tf_op jit(solution)/shard_map/ppermute | solution.py:512
  217.8 41.1 %collective-permute-start.39 = (bf16[4,64,768]{2,1,0:T(8,128)(2,1)S(1)}, bf16[4,64,768]{2,1,0:T(8,128)(2,1)S(1)}, u32[]{:S(2)}, u32[]{:S(2)}) collective-permute-start(bf16[4,64,768]{2,1,0:T(8,128)(2,1)S(1)} %collective-permute-done.38.refs_4_), channel_id=1, source_target_pairs={{0,4},{1,5},{2,6},{3,7},{4,0},{5,1},{6,2},{7,3},{8,12},{9,13},{10,... | collective-permute-start | bytes 1179656 | tf_op jit(solution)/shard_map/ppermute | solution.py:512
  218.1 40.8 %collective-permute-start.37 = (bf16[4,64,768]{2,1,0:T(8,128)(2,1)S(1)}, bf16[4,64,768]{2,1,0:T(8,128)(2,1)S(1)}, u32[]{:S(2)}, u32[]{:S(2)}) collective-permute-start(bf16[4,64,768]{2,1,0:T(8,128)(2,1)S(1)} %collective-permute-done.36.refs_2_), channel_id=1, source_target_pairs={{0,4},{1,5},{2,6},{3,7},{4,0},{5,1},{6,2},{7,3},{8,12},{9,13},{10,... | collective-permute-start | bytes 1179656 | tf_op jit(solution)/shard_map/ppermute | solution.py:512
  400.6 48.0 %collective-permute-start.58 = (bf16[16,96,768]{2,1,0:T(8,128)(2,1)}, bf16[16,96,768]{2,1,0:T(8,128)(2,1)}, u32[]{:S(2)}, u32[]{:S(2)}) collective-permute-start(bf16[16,96,768]{2,1,0:T(8,128)(2,1)} %get-tuple-element.91), channel_id=1, source_target_pairs={{0,4},{1,5},{2,6},{3,7},{4,0},{5,1},{6,2},{7,3},{8,12},{9,13},{10,... | collective-permute-start | bytes 7077896 | tf_op jit(solution)/shard_map/ppermute | solution.py:512
  424.4 29.4 %collective-permute-start.42 = (bf16[16,24,3200]{2,1,0:T(8,128)(2,1)}, bf16[16,24,3200]{2,1,0:T(8,128)(2,1)S(1)}, u32[]{:S(2)}, u32[]{:S(2)}) collective-permute-start(bf16[16,24,3200]{2,1,0:T(8,128)(2,1)} %get-tuple-element.82), channel_id=1, source_target_pairs={{0,4},{1,5},{2,6},{3,7},{4,0},{5,1},{6,2},{7,3},{8,12},{9,13},{10,... | collective-permute-start | bytes 7372808 | tf_op jit(solution)/shard_map/ppermute | solution.py:512
  448.2 22.2 %collective-permute-start.50 = (bf16[16,24,3840]{2,1,0:T(8,128)(2,1)}, bf16[16,24,3840]{2,1,0:T(8,128)(2,1)S(1)}, u32[]{:S(2)}, u32[]{:S(2)}) collective-permute-start(bf16[16,24,3840]{2,1,0:T(8,128)(2,1)} %get-tuple-element.87), channel_id=1, source_target_pairs={{0,4},{1,5},{2,6},{3,7},{4,0},{5,1},{6,2},{7,3},{8,12},{9,13},{10,... | collective-permute-start | bytes 8847368 | tf_op jit(solution)/shard_map/ppermute | solution.py:512
  454.4 26.7 %collective-permute-start.46 = (bf16[4,24,3200]{2,1,0:T(8,128)(2,1)S(1)}, bf16[4,24,3200]{2,1,0:T(8,128)(2,1)S(1)}, u32[]{:S(2)}, u32[]{:S(2)}) collective-permute-start(bf16[4,24,3200]{2,1,0:T(8,128)(2,1)S(1)} %get-tuple-element.107), channel_id=1, source_target_pairs={{0,2},{1,3},{2,0},{3,1},{4,6},{5,7},{6,4},{7,5},{8,10},{9,11},{10,... | collective-permute-start | bytes 1843208 | tf_op jit(solution)/shard_map/ppermute | solution.py:512
  455.9 26.8 %collective-permute-start.43 = (bf16[4,24,3200]{2,1,0:T(8,128)(2,1)S(1)}, bf16[4,24,3200]{2,1,0:T(8,128)(2,1)S(1)}, u32[]{:S(2)}, u32[]{:S(2)}) collective-permute-start(bf16[4,24,3200]{2,1,0:T(8,128)(2,1)S(1)} %get-tuple-element.109), channel_id=1, source_target_pairs={{0,1},{1,0},{2,3},{3,2},{4,5},{5,4},{6,7},{7,6},{8,9},{9,8},{10,11... | collective-permute-start | bytes 1843208 | tf_op jit(solution)/shard_map/ppermute | solution.py:512
  468.1 20.9 %collective-permute-start.63 = (bf16[2,96,768]{2,1,0:T(8,128)(2,1)S(1)}, bf16[2,96,768]{2,1,0:T(8,128)(2,1)S(1)}, u32[]{:S(2)}, u32[]{:S(2)}) collective-permute-start(bf16[2,96,768]{2,1,0:T(8,128)(2,1)S(1)} %get-tuple-element.127), channel_id=1, source_target_pairs={{0,1},{1,0},{2,3},{3,2},{4,5},{5,4},{6,7},{7,6},{8,9},{9,8},{10,11... | collective-permute-start | bytes 884744 | tf_op jit(solution)/shard_map/ppermute | solution.py:512
  471.2 62.6 %collective-permute-start.54 = (bf16[4,24,3840]{2,1,0:T(8,128)(2,1)S(1)}, bf16[4,24,3840]{2,1,0:T(8,128)(2,1)S(1)}, u32[]{:S(2)}, u32[]{:S(2)}) collective-permute-start(bf16[4,24,3840]{2,1,0:T(8,128)(2,1)S(1)} %get-tuple-element.103), channel_id=1, source_target_pairs={{0,2},{1,3},{2,0},{3,1},{4,6},{5,7},{6,4},{7,5},{8,10},{9,11},{10,... | collective-permute-start | bytes 2211848 | tf_op jit(solution)/shard_map/ppermute | solution.py:512
  481.1 53.1 %collective-permute-start.51 = (bf16[4,24,3840]{2,1,0:T(8,128)(2,1)S(1)}, bf16[4,24,3840]{2,1,0:T(8,128)(2,1)S(1)}, u32[]{:S(2)}, u32[]{:S(2)}) collective-permute-start(bf16[4,24,3840]{2,1,0:T(8,128)(2,1)S(1)} %get-tuple-element.105), channel_id=1, source_target_pairs={{0,1},{1,0},{2,3},{3,2},{4,5},{5,4},{6,7},{7,6},{8,9},{9,8},{10,11... | collective-permute-start | bytes 2211848 | tf_op jit(solution)/shard_map/ppermute | solution.py:512
  482.7 27.8 %collective-permute-start.47 = (bf16[2,24,3200]{2,1,0:T(8,128)(2,1)S(1)}, bf16[2,24,3200]{2,1,0:T(8,128)(2,1)S(1)}, u32[]{:S(2)}, u32[]{:S(2)}) collective-permute-start(bf16[2,24,3200]{2,1,0:T(8,128)(2,1)S(1)} %get-tuple-element.123), channel_id=1, source_target_pairs={{0,1},{1,0},{2,3},{3,2},{4,5},{5,4},{6,7},{7,6},{8,9},{9,8},{10,11... | collective-permute-start | bytes 921608 | tf_op jit(solution)/shard_map/ppermute | solution.py:512
  488.9 21.7 %collective-permute-start.44 = (bf16[2,24,3200]{2,1,0:T(8,128)(2,1)S(1)}, bf16[2,24,3200]{2,1,0:T(8,128)(2,1)S(1)}, u32[]{:S(2)}, u32[]{:S(2)}) collective-permute-start(bf16[2,24,3200]{2,1,0:T(8,128)(2,1)S(1)} %get-tuple-element.121), channel_id=1, source_target_pairs={{0,2},{1,3},{2,0},{3,1},{4,6},{5,7},{6,4},{7,5},{8,10},{9,11},{10,... | collective-permute-start | bytes 921608 | tf_op jit(solution)/shard_map/ppermute | solution.py:512
  489.5 23.2 %collective-permute-start.64 = (bf16[96,768]{1,0:T(8,128)(2,1)S(1)}, bf16[96,768]{1,0:T(8,128)(2,1)S(1)}, u32[]{:S(2)}, u32[]{:S(2)}) collective-permute-start(bf16[96,768]{1,0:T(8,128)(2,1)S(1)} %get-tuple-element.132), channel_id=1, source_target_pairs={{0,16},{1,17},{2,18},{3,19},{4,20},{5,21},{6,22},{7,23},{8,24},{9,... | collective-permute-start | bytes 442376 | tf_op jit(solution)/shard_map/ppermute | solution.py:512
  (63 other events, 1087.7 us)
